TPU v7x, 512 devices: a whole 4x4x16 slice. The times are simulated.
512 devices in a mesh: ctx: 64 (over z, x_hi, core), head: 8 (over x_lo, y).
Axes of the slice: x: 4 (x_hi: 2, x_lo: 2; x = x_hi * 2 + x_lo), y: 4, z: 16, core: 2. Of those that a mesh axis runs over, the one named last changes fastest.
Arguments:
- queries: bfloat16 [16384, 4096], P('ctx', 'head'), may hold values from -6 to 6
- key_rows: bfloat16 [16384, 1024], P('ctx', 'head'), may hold values from -6 to 6
- value_rows: bfloat16 [16384, 1024], P('ctx', 'head'), may hold values from -6 to 6
- attn_out: bfloat16 [16384, 4096], P('ctx', 'head'), may hold values from -6 to 6
- out_grad: bfloat16 [16384, 4096], P('ctx', 'head'), may hold values from -6 to 6
- log_sums: float32 [32, 16384], P('head', 'ctx'), may hold values from 4.5 to 6
- block_picks: int32 [128, 32, 3], P('ctx', 'head'), may hold values from 0 to 3, all different within a row
- query_weight: bfloat16 [4096, 4096], P('ctx', 'head'), may hold values from -0.21875 to 0.21875
- key_weight: bfloat16 [4096, 1024], P('ctx', 'head'), may hold values from -0.21875 to 0.21875
- value_weight: bfloat16 [4096, 1024], P('ctx', 'head'), may hold values from -0.21875 to 0.21875
Outputs:
- input_grad: bfloat16 [16384, 4096], P('ctx', 'head')
Inputs may be any that keep to these rules, and one draw needn't show every extreme that they name: `block_picks`: in each row (query block, query head) the 3 entries differ; entry m selects the block m + 1 blocks before the query's block, and selections before the sequence's start select nothing.
All inputs are finite; a program needn't handle non-finite values.
Results may differ from a plain program's by a relative error of at most 0.013.
Values may be sent and summed in bfloat16 or wider, within the bound.
No kernel may reach another device: no remote copies, remote signals or barrier semaphores. Data moves between devices by JAX's collectives and lax.ppermute only.
A program may use at most 64 MiB of HBM per device.

v0:
```python
import math

import jax
import jax.numpy as jnp
from jax import lax
from jax.sharding import PartitionSpec as P

BLK = 128


def passed_along(x, axis, by):
    devices = lax.axis_size(axis)
    pairs = [(i, i + by) for i in range(devices) if 0 <= i + by < devices]
    return lax.ppermute(x, axis, pairs)


def block_grads(
    query_blocks,
    grad_blocks,
    log_part,
    delta_part,
    pick_part,
    query_first,
    key_table,
    value_table,
    key_first,
):
    blocks, width, group, head_dim = query_blocks.shape
    table_blocks = key_table.shape[0]
    scaling = 1.0 / math.sqrt(head_dim)
    offsets = jnp.concatenate([jnp.zeros((blocks, group, 1), jnp.int32), pick_part + 1], axis=2)
    query_ids = query_first + jnp.arange(blocks, dtype=jnp.int32)
    key_block = query_ids[:, None, None] - offsets
    table_index = key_block - key_first
    usable = (table_index >= 0) & (table_index < table_blocks) & (key_block >= 0)
    clipped = jnp.clip(table_index, 0, table_blocks - 1)
    key_sel = key_table[clipped]
    value_sel = value_table[clipped]
    scores = (
        jnp.einsum("bqgd,bgskd->bgqsk", query_blocks, key_sel, preferred_element_type=jnp.float32)
        * scaling
    )
    position = jnp.arange(width)
    causal = position[:, None] >= position[None, :]
    allowed = usable[:, :, None, :, None] & (
        (offsets != 0)[:, :, None, :, None] | causal[None, None, :, None, :]
    )
    probability = jnp.where(allowed, jnp.exp(scores - log_part[:, :, :, None, None]), 0.0)
    prob_grad = jnp.einsum(
        "bqgd,bgskd->bgqsk", grad_blocks, value_sel, preferred_element_type=jnp.float32
    )
    score_grad = probability * (prob_grad - delta_part[:, :, :, None, None])
    prob_half = probability.astype(jnp.bfloat16)
    grad_half = score_grad.astype(jnp.bfloat16)
    query_grad = (
        jnp.einsum("bgqsk,bgskd->bqgd", grad_half, key_sel, preferred_element_type=jnp.float32)
        * scaling
    )
    key_terms = (
        jnp.einsum("bgqsk,bqgd->bgskd", grad_half, query_blocks, preferred_element_type=jnp.float32)
        * scaling
    )
    value_terms = jnp.einsum(
        "bgqsk,bqgd->bgskd", prob_half, grad_blocks, preferred_element_type=jnp.float32
    )
    onehot = (usable[..., None] & (clipped[..., None] == jnp.arange(table_blocks))).astype(
        jnp.float32
    )
    key_grad = jnp.einsum("bgsc,bgskd->ckd", onehot, key_terms, precision=lax.Precision.HIGHEST)
    value_grad = jnp.einsum("bgsc,bgskd->ckd", onehot, value_terms, precision=lax.Precision.HIGHEST)
    return (query_grad, key_grad, value_grad)


def per_device(
    queries,
    key_rows,
    value_rows,
    attn_out,
    out_grad,
    log_sums,
    block_picks,
    query_weight,
    key_weight,
    value_weight,
):
    tokens, query_cols = queries.shape
    head_dim = key_rows.shape[1]
    group = query_cols // head_dim
    width = BLK
    blocks = tokens // width
    cycle_pos = lax.axis_index("ctx")
    own_first = cycle_pos * blocks
    query_blocks = queries.reshape(blocks, width, group, head_dim)
    grad_blocks = out_grad.reshape(blocks, width, group, head_dim)
    delta_part = jnp.sum(
        (out_grad.astype(jnp.float32) * attn_out.astype(jnp.float32)).reshape(
            blocks, width, group, head_dim
        ),
        axis=3,
    ).transpose(0, 2, 1)
    log_part = log_sums.reshape(group, blocks, width).transpose(1, 0, 2)
    fetched = []
    for distance in (1, 2):
        fetched.append(passed_along((key_rows, value_rows), "ctx", distance))
    key_table = jnp.concatenate([fetched[1][0], fetched[0][0], key_rows], axis=0).reshape(
        3 * blocks, width, head_dim
    )
    value_table = jnp.concatenate([fetched[1][1], fetched[0][1], value_rows], axis=0).reshape(
        3 * blocks, width, head_dim
    )
    query_grad, key_grad, value_grad = block_grads(
        query_blocks,
        grad_blocks,
        log_part,
        delta_part,
        block_picks,
        own_first,
        key_table,
        value_table,
        own_first - 2 * blocks,
    )
    key_own = key_grad[2 * blocks :]
    value_own = value_grad[2 * blocks :]
    for distance in (1, 2):
        lower = (2 - distance) * blocks
        returned = passed_along(
            (key_grad[lower : lower + blocks], value_grad[lower : lower + blocks]), "ctx", -distance
        )
        key_own = key_own + returned[0]
        value_own = value_own + returned[1]
    grads = jnp.concatenate(
        [
            query_grad.reshape(tokens, query_cols).astype(jnp.bfloat16),
            key_own.reshape(tokens, head_dim).astype(jnp.bfloat16),
            value_own.reshape(tokens, head_dim).astype(jnp.bfloat16),
        ],
        axis=1,
    )
    weight_cat = jnp.concatenate([query_weight, key_weight, value_weight], axis=1)
    partial_value = lax.dot_general(
        grads,
        lax.all_gather(weight_cat, "ctx", axis=0, tiled=True),
        (((1,), (1,)), ((), ())),
        preferred_element_type=jnp.float32,
    )
    return lax.psum_scatter(
        partial_value.astype(jnp.bfloat16), "head", scatter_dimension=1, tiled=True
    )


def solution(mesh):
    placed = (
        P("ctx", "head"),
        P("ctx", "head"),
        P("ctx", "head"),
        P("ctx", "head"),
        P("ctx", "head"),
        P("head", "ctx"),
        P("ctx", "head", None),
        P("ctx", "head"),
        P("ctx", "head"),
        P("ctx", "head"),
    )
    return jax.shard_map(
        per_device, mesh=mesh, in_specs=placed, out_specs=P("ctx", "head"), check_vma=False
    )
```

profile of v0, /device:TPU:4, one launch (start us, length us, event | category | flops | bytes accessed | tf_op | source)
XLA Modules:
  0.0 230.7 jit_solution(6480486702893773419)
XLA Ops:
  6.5 0.0 all-gather.2.cloned.1.call-start
  6.5 1.5 pad_maximum_fusion.2
  8.1 0.0 copy-start
  8.1 0.0 all-gather.2.cloned.1.call-update
  8.1 0.0 reduce-scatter.2.cloned.1.call-start
  8.1 3.8 %collective-permute-start = (bf16[256,128]{1,0:T(8,128)(2,1)}, bf16[256,128]{1,0:T(8,128)(2,1)S(1)}, u32[]{:S(2)}, u32[]{:S(2)}) collective-permute-start(bf16[256,128]{1,0:T(8,128)(2,1)} %param.11), channel_id=1, source_target_pairs={{0,16},{8,24},{16,32},{24,40},{32,48},{40,56},{48,64},{56,72},{64,... | collective-permute-start | bytes 196616 | tf_op jit(solution)/shard_map/ppermute | solution.py:14
  11.9 1.9 collective-permute-start.1
  13.8 4.9 %collective-permute-start.2 = (bf16[256,128]{1,0:T(8,128)(2,1)}, bf16[256,128]{1,0:T(8,128)(2,1)S(1)}, u32[]{:S(2)}, u32[]{:S(2)}) collective-permute-start(bf16[256,128]{1,0:T(8,128)(2,1)} %param.12), channel_id=1, source_target_pairs={{0,16},{8,24},{16,32},{24,40},{32,48},{40,56},{48,64},{56,72},{64,... | collective-permute-start | bytes 196616 | tf_op jit(solution)/shard_map/ppermute | solution.py:14
  18.8 3.6 %collective-permute-start.3 = (bf16[256,128]{1,0:T(8,128)(2,1)}, bf16[256,128]{1,0:T(8,128)(2,1)S(1)}, u32[]{:S(2)}, u32[]{:S(2)}) collective-permute-start(bf16[256,128]{1,0:T(8,128)(2,1)} %param.12), channel_id=1, source_target_pairs={{0,8},{8,16},{16,24},{24,32},{32,40},{40,48},{48,56},{56,64},{64,7... | collective-permute-start | bytes 196616 | tf_op jit(solution)/shard_map/ppermute | solution.py:14
  22.4 0.7 broadcast_add_fusion
  23.1 0.1 compare_select_fusion
  23.2 0.1 copy.38
  23.3 0.1 reshape.54
  23.4 0.1 compare_and_fusion
  23.4 0.1 copy.40
  23.6 0.1 copy.41
  23.7 1.0 reshape.47
  24.7 1.0 reshape.50
  25.7 1.1 convert_multiply_fusion
  26.8 0.0 copy-start.1
  26.8 0.2 reshape.51
  27.0 0.3 reduce_sum.9
  27.4 0.1 copy.46
  27.4 0.1 copy.50
  27.6 0.0 collective-permute-done
  27.6 0.0 collective-permute-done.1
  27.6 0.0 copy-done
  27.6 0.0 copy-start.2
  27.7 0.7 gather_fusion
  28.4 0.0 collective-permute-done.2
  28.4 0.0 collective-permute-done.3
  28.4 0.0 copy-done.1
  28.5 0.7 gather_fusion.1
  29.2 0.0 copy-done.2
  29.2 0.7 bitcast_select_fusion
  30.0 0.5 fusion
  30.4 0.4 convolution_multiply_fusion
  30.9 3.3 %fusion.5 = f32[6,128,128]{2,0,1:T(8,128)S(1)} fusion(f32[2,4,4,128,128]{4,3,2,1,0:T(8,128)S(1)} %convolution_multiply_fusion, s32[2,4,4]{2,1,0:T(4,128)S(1)} %copy.50, pred[2,4,4]{2,1,0:T(4,128)(4,1)S(1)} %copy.40), kind=kOutput, calls=%fused_computation.11 | convolution fusion | flops 37749120 | bytes 2490528 | tf_op jit(solution)/shard_map/bgsc,bgskd->ckd/dot_general | solution.py:69
  34.2 0.1 fusion.34
  34.3 3.5 %collective-permute-start.4 = (f32[2,128,128]{2,0,1:T(2,128)S(1)}, f32[2,128,128]{2,0,1:T(2,128)S(1)}, u32[]{:S(2)}, u32[]{:S(2)}) collective-permute-start(f32[2,128,128]{2,0,1:T(2,128)S(1)} %get-tuple-element.7), channel_id=1, source_target_pairs={{8,0},{16,8},{24,16},{32,24},{40,32},{48,40},{56,48},{64,56},{72,6... | collective-permute-start | bytes 393224 | tf_op jit(solution)/shard_map/ppermute | solution.py:14
  37.8 1.9 collective-permute-start.5
  39.7 0.4 fusion.14
  40.1 3.3 %fusion.8 = f32[6,128,128]{2,0,1:T(8,128)S(1)} fusion(f32[2,4,4,128,128]{4,3,2,1,0:T(8,128)S(1)} %fusion.14, s32[2,4,4]{2,1,0:T(4,128)S(1)} %copy.50, pred[2,4,4]{2,1,0:T(4,128)(4,1)S(1)} %copy.40), kind=kOutput, calls=%fused_computation.12 | convolution fusion | flops 37749120 | bytes 2490528 | tf_op jit(solution)/shard_map/bgsc,bgskd->ckd/dot_general | solution.py:70
  43.4 0.5 fusion.13
  43.9 0.1 fusion.35
  44.0 1.9 collective-permute-start.6
  46.0 1.9 collective-permute-start.7
  47.9 0.2 copy.48
  48.1 0.0 collective-permute-done.4
  48.2 0.0 collective-permute-done.5
  48.2 0.1 fusion.28
  48.3 0.1 collective-permute-done.6
  48.5 8.6 %collective-permute-done.7 = f32[2,128,128]{2,0,1:T(2,128)S(1)} collective-permute-done((f32[2,128,128]{2,0,1:T(2,128)S(1)}, f32[2,128,128]{2,0,1:T(2,128)S(1)}, u32[]{:S(2)}, u32[]{:S(2)}) %collective-permute-start.7) | collective-permute-done | bytes 131104 | tf_op jit(solution)/shard_map/ppermute | solution.py:14
  57.1 0.1 fusion.26
  57.2 113.4 %all-gather.2.cloned.1.call-done = bf16[4096,768]{1,0:T(8,128)(2,1)} async-done(((bf16[64,768]{1,0:T(8,128)(2,1)}), bf16[4096,768]{1,0:T(8,128)(2,1)}) %all-gather.2.cloned.1.call-update) | async-done | bytes 6291472 | tf_op jit(solution)/shard_map/all_gather | solution.py:142
  170.6 6.0 %convolution_convert_fusion = bf16[256,4096]{1,0:T(8,128)(2,1)} fusion(bf16[4096,768]{1,0:T(8,128)(2,1)} %all-gather.2.cloned.1.call-done, bf16[256,128]{1,0:T(8,128)(2,1)S(1)} %bitcast.71, bf16[256,128]{1,0:T(8,128)(2,1)S(1)} %bitcast.70, bf16[256,512]{1,0:T(8,128)(2,1)S(1)} %bitcast.69), kind=kOutput, calls=%fused_computation.2 | convolution fusion | flops 1612840960 | bytes 8781824 | tf_op jit(solution)/shard_map/dot_general | solution.py:140
  176.6 0.0 reduce-scatter.2.cloned.1.call-update
  176.6 47.3 %reduce-scatter.2.cloned.1.call-done = bf16[256,512]{1,0:T(8,128)(2,1)} async-done(((bf16[256,4096]{1,0:T(8,128)(2,1)}), bf16[256,512]{1,0:T(8,128)(2,1)}) %reduce-scatter.2.cloned.1.call-update) | async-done | bytes 262160 | tf_op jit(solution)/shard_map/reduce_scatter | solution.py:146
  (8 shorter events, 0.1 us)
Async XLA Ops:
  6.5 164.1 %all-gather.2.cloned.1.call-start = ((), (), s32[]{:S(2)}) async-start(), calls=%async_computation.1 | async-start | bytes 6389760 | tf_op jit(solution)/shard_map/all_gather | solution.py:142
  8.1 19.6 %copy-start = (bf16[256,128]{1,0:T(8,128)(2,1)S(1)}, bf16[256,128]{1,0:T(8,128)(2,1)}, u32[]{:S(2)}) copy-start(bf16[256,128]{1,0:T(8,128)(2,1)} %param.11) | copy-start | bytes 196612
  8.1 215.8 %reduce-scatter.2.cloned.1.call-start = ((), (), s32[]{:S(2)}) async-start(), calls=%async_computation.2 | async-start | bytes 2359296 | tf_op jit(solution)/shard_map/reduce_scatter | solution.py:146
  8.1 19.5 %collective-permute-start = (bf16[256,128]{1,0:T(8,128)(2,1)}, bf16[256,128]{1,0:T(8,128)(2,1)S(1)}, u32[]{:S(2)}, u32[]{:S(2)}) collective-permute-start(bf16[256,128]{1,0:T(8,128)(2,1)} %param.11), channel_id=1, source_target_pairs={{0,16},{8,24},{16,32},{24,40},{32,48},{40,56},{48,64},{56,72},{64,... | collective-permute-start | bytes 196616 | tf_op jit(solution)/shard_map/ppermute | solution.py:14
  11.9 15.7 %collective-permute-start.1 = (bf16[256,128]{1,0:T(8,128)(2,1)}, bf16[256,128]{1,0:T(8,128)(2,1)S(1)}, u32[]{:S(2)}, u32[]{:S(2)}) collective-permute-start(bf16[256,128]{1,0:T(8,128)(2,1)} %param.11), channel_id=1, source_target_pairs={{0,8},{8,16},{16,24},{24,32},{32,40},{40,48},{48,56},{56,64},{64,7... | collective-permute-start | bytes 196616 | tf_op jit(solution)/shard_map/ppermute | solution.py:14
  13.8 14.6 %collective-permute-start.2 = (bf16[256,128]{1,0:T(8,128)(2,1)}, bf16[256,128]{1,0:T(8,128)(2,1)S(1)}, u32[]{:S(2)}, u32[]{:S(2)}) collective-permute-start(bf16[256,128]{1,0:T(8,128)(2,1)} %param.12), channel_id=1, source_target_pairs={{0,16},{8,24},{16,32},{24,40},{32,48},{40,56},{48,64},{56,72},{64,... | collective-permute-start | bytes 196616 | tf_op jit(solution)/shard_map/ppermute | solution.py:14
  18.8 9.6 %collective-permute-start.3 = (bf16[256,128]{1,0:T(8,128)(2,1)}, bf16[256,128]{1,0:T(8,128)(2,1)S(1)}, u32[]{:S(2)}, u32[]{:S(2)}) collective-permute-start(bf16[256,128]{1,0:T(8,128)(2,1)} %param.12), channel_id=1, source_target_pairs={{0,8},{8,16},{16,24},{24,32},{32,40},{40,48},{48,56},{56,64},{64,7... | collective-permute-start | bytes 196616 | tf_op jit(solution)/shard_map/ppermute | solution.py:14
  26.8 1.6 copy-start.1
  27.6 1.6 copy-start.2
  34.3 13.9 %collective-permute-start.4 = (f32[2,128,128]{2,0,1:T(2,128)S(1)}, f32[2,128,128]{2,0,1:T(2,128)S(1)}, u32[]{:S(2)}, u32[]{:S(2)}) collective-permute-start(f32[2,128,128]{2,0,1:T(2,128)S(1)} %get-tuple-element.7), channel_id=1, source_target_pairs={{8,0},{16,8},{24,16},{32,24},{40,32},{48,40},{56,48},{64,56},{72,6... | collective-permute-start | bytes 393224 | tf_op jit(solution)/shard_map/ppermute | solution.py:14
  37.8 10.4 %collective-permute-start.5 = (f32[2,128,128]{2,0,1:T(2,128)S(1)}, f32[2,128,128]{2,0,1:T(2,128)S(1)}, u32[]{:S(2)}, u32[]{:S(2)}) collective-permute-start(f32[2,128,128]{2,0,1:T(2,128)S(1)} %get-tuple-element.8), channel_id=1, source_target_pairs={{16,0},{24,8},{32,16},{40,24},{48,32},{56,40},{64,48},{72,56},{80,... | collective-permute-start | bytes 393224 | tf_op jit(solution)/shard_map/ppermute | solution.py:14
  44.0 4.4 %collective-permute-start.6 = (f32[2,128,128]{2,0,1:T(2,128)S(1)}, f32[2,128,128]{2,0,1:T(2,128)S(1)}, u32[]{:S(2)}, u32[]{:S(2)}) collective-permute-start(f32[2,128,128]{2,0,1:T(2,128)S(1)} %get-tuple-element.9), channel_id=1, source_target_pairs={{8,0},{16,8},{24,16},{32,24},{40,32},{48,40},{56,48},{64,56},{72,6... | collective-permute-start | bytes 393224 | tf_op jit(solution)/shard_map/ppermute | solution.py:14
  46.0 11.1 %collective-permute-start.7 = (f32[2,128,128]{2,0,1:T(2,128)S(1)}, f32[2,128,128]{2,0,1:T(2,128)S(1)}, u32[]{:S(2)}, u32[]{:S(2)}) collective-permute-start(f32[2,128,128]{2,0,1:T(2,128)S(1)} %get-tuple-element.10), channel_id=1, source_target_pairs={{16,0},{24,8},{32,16},{40,24},{48,32},{56,40},{64,48},{72,56},{80,... | collective-permute-start | bytes 393224 | tf_op jit(solution)/shard_map/ppermute | solution.py:14
Sparse Core Ops, SparseCore 0:
  10.6 159.9 all-gather.1
  176.7 47.1 reduce-scatter.1
where the time goes:
time: 231 us
  waiting for transfers between devices  169 us (73%)
  starting transfers between devices  23.5 us (10%)
  matrix products  15.1 us (7%)
  between operations  13.7 us (6%)
  local copies, waits for them, and re-layouts  4.78 us (2%)
  other arithmetic  4.14 us (2%)
    all_gather x1, waiting for transfers between devices, per_device(): lax.all_gather(weight_cat, 'ctx', axis=0, tiled=True)  113 us
    reduce_scatter x1, waiting for transfers between devices, per_device(): lax.psum_scatter(partial_value.astype(jnp.bfloat16), 'head', scatter_dime...  47.3 us
    ppermute x8, starting transfers between devices, passed_along(): return lax.ppermute(x, axis, pairs)  23.5 us
    ppermute x8, waiting for transfers between devices, passed_along(): return lax.ppermute(x, axis, pairs)  8.79 us
    dot_general x1, matrix products, per_device(): lax.dot_general(grads, lax.all_gather(weight_cat, 'ctx', axis=0, tiled=Tr...  5.96 us
  transfers between devices with their start and end apart: 10, of which 4 were waited for; matrix products, arithmetic and copies ran while one was open for 7% of the time, Pallas kernels for 0%

commit v1 on v0

v1 whole, which is shorter than its diff:
```python
import math

import jax
import jax.numpy as jnp
from jax import lax
from jax.experimental import pallas as pl
from jax.experimental.pallas import tpu as pltpu
from jax.sharding import Mesh
from jax.sharding import PartitionSpec as P


BLK = 128
HD = 128
GROUP = 4
BF = jnp.bfloat16
F32 = jnp.float32
Z = ("zh", "zl")
CTX = ("zh", "zl", "xh", "core")
HEAD = ("xl", "y")
NT = (((1,), (1,)), ((), ()))
NN = (((1,), (0,)), ((), ()))
TN = (((0,), (0,)), ((), ()))


def dot(a, b, dims):
    return lax.dot_general(a, b, dims, preferred_element_type=F32)


def passed_along(x, axis, by):
    n = lax.axis_size(axis)
    pairs = [(i, i + by) for i in range(n) if 0 <= i + by < n]
    return lax.ppermute(x, axis, pairs)


def shifted(x, axis, by):
    n = lax.axis_size(axis)
    return lax.ppermute(x, axis, [(i, (i + by) % n) for i in range(n)])


def attention_kernel(
    where_ref, picks_ref, q_ref, do_ref, o_ref, lse_ref, kv0_ref, kv1_ref, kv2_ref,
    aq_ref, own_ref, ret1_ref, ret2_ref,
):
    scaling = 1.0 / math.sqrt(HD)
    first = where_ref[0] * 2
    tables = (kv2_ref, kv2_ref, kv1_ref, kv1_ref, kv0_ref, kv0_ref)
    sums = (ret2_ref, ret2_ref, ret1_ref, ret1_ref, own_ref, own_ref)
    key_at = lax.broadcasted_iota(jnp.int32, (BLK, BLK), 0)
    query_at = lax.broadcasted_iota(jnp.int32, (BLK, BLK), 1)
    causal = key_at <= query_at
    dk = [None] * 6
    dv = [None] * 6
    for b in range(2):
        rows = slice(BLK * b, BLK * b + BLK)
        cols = [slice(HD * h, HD * h + HD) for h in range(GROUP)]
        q = jnp.concatenate([q_ref[rows, c] for c in cols], axis=0)
        do = jnp.concatenate([do_ref[rows, c] for c in cols], axis=0)
        lse = []
        delta = []
        for h in range(GROUP):
            prod = do_ref[rows, cols[h]].astype(F32) * o_ref[rows, cols[h]].astype(F32)
            delta.append(jnp.sum(prod.T, axis=0, keepdims=True))
            lse.append(lse_ref[h : h + 1, rows])
        dq = None
        for s in range(5):
            c = b + s
            half = slice(BLK * (c % 2), BLK * (c % 2) + BLK)
            k = tables[c][half, :HD]
            v = tables[c][half, HD:]
            scores = dot(k, q, NT)
            prob_grad = dot(v, do, NT)
            p_parts = []
            g_parts = []
            for h in range(GROUP):
                at = slice(BLK * h, BLK * h + BLK)
                p = jnp.exp(scores[:, at] * scaling - lse[h])
                if s == 4:
                    p = jnp.where(causal, p, 0.0)
                else:
                    m = 3 - s
                    used = picks_ref[b, h, 0] == m
                    for t in range(1, 3):
                        used = used | (picks_ref[b, h, t] == m)
                    used = used & (first + b - 1 - m >= 0)
                    p = jnp.where(used, p, 0.0)
                p_parts.append(p.astype(BF))
                g_parts.append((p * (prob_grad[:, at] - delta[h])).astype(BF))
            p_half = jnp.concatenate(p_parts, axis=1)
            g_half = jnp.concatenate(g_parts, axis=1)
            part = dot(g_half, k, TN)
            dq = part if dq is None else dq + part
            k_part = dot(g_half, q, NN)
            v_part = dot(p_half, do, NN)
            dk[c] = k_part if dk[c] is None else dk[c] + k_part
            dv[c] = v_part if dv[c] is None else dv[c] + v_part
        for h in range(GROUP):
            aq_ref[rows, cols[h]] = (dq[BLK * h : BLK * h + BLK] * scaling).astype(BF)
    for c in range(6):
        half = slice(BLK * (c % 2), BLK * (c % 2) + BLK)
        sums[c][half, :HD] = (dk[c] * scaling).astype(sums[c].dtype)
        sums[c][half, HD:] = dv[c].astype(sums[c].dtype)


def attention(where, picks, q, do, o, lse, kv0, kv1, kv2):
    tokens = q.shape[0]
    vm = pl.BlockSpec(memory_space=pltpu.VMEM)
    sm = pl.BlockSpec(memory_space=pltpu.SMEM)
    return pl.pallas_call(
        attention_kernel,
        out_shape=(
            jax.ShapeDtypeStruct(q.shape, BF),
            jax.ShapeDtypeStruct((tokens, 2 * HD), F32),
            jax.ShapeDtypeStruct((tokens, 2 * HD), BF),
            jax.ShapeDtypeStruct((tokens, 2 * HD), BF),
        ),
        in_specs=[sm, sm] + [vm] * 7,
        out_specs=(vm,) * 4,
        name="attention",
    )(where, picks, q, do, o, lse, kv0, kv1, kv2)


def project_kernel(where_ref, aq_ref, akv_ref, wc_ref, wo_ref, out_ref):
    zl = where_ref[1]
    core = where_ref[2]
    for head in range(8):
        zh = head // 2
        wide = []
        for e in range(2):
            k = lax.rem(2 * (head % 2) + e + 4 - zl, 4)
            mine = wc_ref[k, zh]
            other = wo_ref[k, zh]
            wide.append(jnp.where(core == 0, mine, other))
            wide.append(jnp.where(core == 0, other, mine))
        w = jnp.concatenate(wide, axis=0)
        for r in range(2):
            total = dot(aq_ref[r], w[:, : GROUP * HD], NT) + dot(akv_ref[r], w[:, GROUP * HD :], NT)
            out_ref[8 * r + head] = total.astype(BF)


def project(where, aq, akv, wc, wo):
    vm = pl.BlockSpec(memory_space=pltpu.VMEM)
    return pl.pallas_call(
        project_kernel,
        out_shape=jax.ShapeDtypeStruct((16, aq.shape[1], 256), BF),
        in_specs=[pl.BlockSpec(memory_space=pltpu.SMEM)] + [vm] * 4,
        out_specs=vm,
        name="project",
    )(where, aq, akv, wc, wo)


def total_kernel(in_ref, out_ref):
    for xh in range(2):
        total = in_ref[8 * xh].astype(F32)
        for h in range(1, 8):
            total = total + in_ref[8 * xh + h].astype(F32)
        for e in range(2):
            at = 256 * e + 128 * xh
            out_ref[:, at : at + 128] = total[:, 128 * e : 128 * e + 128].astype(BF)


def totalled(parts):
    rows = parts.shape[1]
    step = 64
    return pl.pallas_call(
        total_kernel,
        grid=(rows // step,),
        out_shape=jax.ShapeDtypeStruct((rows, 512), BF),
        in_specs=[pl.BlockSpec((16, step, 256), lambda i: (0, i, 0))],
        out_specs=pl.BlockSpec((step, 512), lambda i: (i, 0)),
        name="total",
    )(parts)


def per_device(
    queries, key_rows, value_rows, attn_out, out_grad, log_sums, block_picks,
    query_weight, key_weight, value_weight,
):
    where = jnp.stack(
        [lax.axis_index(CTX), lax.axis_index("zl"), lax.axis_index("core")]
    ).astype(jnp.int32)
    kv0 = jnp.concatenate([key_rows, value_rows], axis=1)
    kv1 = passed_along(kv0, CTX, 1)
    kv2 = passed_along(kv0, CTX, 2)
    weight = jnp.concatenate([query_weight, key_weight, value_weight], axis=1)
    w0 = lax.all_gather(weight, "zh")
    w1 = shifted(w0, Z, -1)
    w3 = shifted(w0, Z, 1)
    w2a = shifted(w0[:2], Z, -2)
    w2b = shifted(w0[2:], Z, 2)
    aq, own, ret1, ret2 = attention(
        where, block_picks, queries, out_grad, attn_out, log_sums, kv0, kv1, kv2
    )
    back1 = passed_along(ret1, CTX, -1)
    back2 = passed_along(ret2, CTX, -2)
    aq_all = lax.all_gather(aq, "xh")
    akv = (own + back1.astype(F32) + back2.astype(F32)).astype(BF)
    akv_all = lax.all_gather(akv, "xh")
    wc = jnp.concatenate([w0, w1, w2a, w2b, w3], axis=0).reshape(4, 4, *weight.shape)
    wo = shifted(wc, "core", 1)
    parts = project(where, aq_all, akv_all, wc, wo)
    parts = lax.all_to_all(parts, ("xh", "xl", "y"), 0, 0)
    return totalled(parts)


def solution(mesh):
    wide = Mesh(
        mesh.devices.reshape(4, 4, 2, 2, 2, 4), ("zh", "zl", "xh", "core", "xl", "y")
    )
    both = P(CTX, HEAD)
    placed = (both,) * 5 + (P(HEAD, CTX), P(CTX, HEAD, None)) + (both,) * 3
    return jax.shard_map(
        per_device, mesh=wide, in_specs=placed, out_specs=both, check_vma=False
    )
```

time: 231 us -> 144 us (0.62)
  the two profiles are of different devices: /device:TPU:4 before, /device:TPU:8 now
where the time goes in v1:
time: 144 us; the launch traced here: 143 us
  blocking collectives  90.1 us (63%)
  starting transfers between devices  24.3 us (17%)
  Pallas kernels  14.1 us (10%)
  waiting for transfers between devices  8.68 us (6%)
  local copies, waits for them, and re-layouts  3.33 us (2%)
  other arithmetic  2.5 us (2%)
    all_to_all x1, blocking collectives, per_device(): parts = lax.all_to_all(parts, ('xh', 'xl', 'y'), 0, 0)  34.5 us
    all_gather x1, blocking collectives, per_device(): w0 = lax.all_gather(weight, 'zh')  30.5 us
    all_gather x1, blocking collectives, per_device(): aq_all = lax.all_gather(aq, 'xh')  16.9 us
    ppermute x5, starting transfers between devices, shifted(): return lax.ppermute(x, axis, [(i, (i + by) % n) for i in range(n)])  14.6 us
    ppermute x4, starting transfers between devices, passed_along(): return lax.ppermute(x, axis, pairs)  9.64 us
    ppermute x5, waiting for transfers between devices, shifted(): return lax.ppermute(x, axis, [(i, (i + by) % n) for i in range(n)])  8.67 us
    all_gather x1, blocking collectives, per_device(): akv_all = lax.all_gather(akv, 'xh')  8.17 us
    pallas_call x1, Pallas kernels, project(): pl.pallas_call(project_kernel, out_shape=jax.ShapeDtypeStruct((16, aq.sha...  5.32 us
  transfers between devices with their start and end apart: 9, of which 3 were waited for; matrix products, arithmetic and copies ran while one was open for 2% of the time, Pallas kernels for 4%

profile of v1, /device:TPU:8, one launch (start us, length us, event | category | flops | bytes accessed | tf_op | source)
XLA Modules:
  0.0 143.2 jit_solution(15525092142278774206)
XLA Ops:
  0.0 0.9 pad_maximum_fusion
  0.9 30.5 %all-gather.2 = bf16[256,768]{1,0:T(8,128)(2,1)S(1)} all-gather(bf16[64,768]{1,0:T(8,128)(2,1)S(1)} %pad_maximum_fusion), channel_id=4, replica_groups=mesh['zh'=4,'zl'=4,'xh'=2,'core'=2,'xl'=2,'y'=4] {'zh'}, dimensions={0}, use_global_device_ids=true | all-gather | bytes 491520 | tf_op jit(solution)/shard_map/all_gather | solution.py:185
  31.4 2.8 %collective-permute-start.4 = (bf16[4,64,768]{2,1,0:T(8,128)(2,1)S(1)}, bf16[4,64,768]{2,1,0:T(8,128)(2,1)S(1)}, u32[]{:S(2)}, u32[]{:S(2)}) collective-permute-start(bf16[4,64,768]{2,1,0:T(8,128)(2,1)S(1)} %bitcast.9), channel_id=1, source_target_pairs={{0,480},{32,0},{64,32},{96,64},{128,96},{160,128},{192,160},{224,1... | collective-permute-start | bytes 1179656 | tf_op jit(solution)/shard_map/ppermute | solution.py:37
  34.2 3.1 %collective-permute-start.7 = (bf16[4,64,768]{2,1,0:T(8,128)(2,1)S(1)}, bf16[4,64,768]{2,1,0:T(8,128)(2,1)S(1)}, u32[]{:S(2)}, u32[]{:S(2)}) collective-permute-start(bf16[4,64,768]{2,1,0:T(8,128)(2,1)S(1)} %bitcast.10), channel_id=1, source_target_pairs={{0,32},{32,64},{64,96},{96,128},{128,160},{160,192},{192,224},{224... | collective-permute-start | bytes 1179656 | tf_op jit(solution)/shard_map/ppermute | solution.py:37
  37.3 3.4 %collective-permute-start.5 = (bf16[2,64,768]{2,1,0:T(8,128)(2,1)S(1)}, bf16[2,64,768]{2,1,0:T(8,128)(2,1)S(1)}, u32[]{:S(2)}, u32[]{:S(2)}) collective-permute-start(bf16[2,64,768]{2,1,0:T(8,128)(2,1)S(1)} %bitcast.17), channel_id=1, source_target_pairs={{0,448},{32,480},{64,0},{96,32},{128,64},{160,96},{192,128},{224,1... | collective-permute-start | bytes 589832 | tf_op jit(solution)/shard_map/ppermute | solution.py:37
  40.7 0.0 copy-start.5
  40.7 0.0 copy-start.6
  40.7 0.0 copy-start.7
  40.7 3.5 %collective-permute-start.6 = (bf16[2,64,768]{2,1,0:T(8,128)(2,1)S(1)}, bf16[2,64,768]{2,1,0:T(8,128)(2,1)S(1)}, u32[]{:S(2)}, u32[]{:S(2)}) collective-permute-start(bf16[2,64,768]{2,1,0:T(8,128)(2,1)S(1)} %bitcast.16), channel_id=1, source_target_pairs={{0,64},{32,96},{64,128},{96,160},{128,192},{160,224},{192,256},{22... | collective-permute-start | bytes 589832 | tf_op jit(solution)/shard_map/ppermute | solution.py:37
  44.2 1.2 collective-permute-done.4
  45.4 4.1 %collective-permute-done.5 = bf16[2,64,768]{2,1,0:T(8,128)(2,1)S(1)} collective-permute-done((bf16[2,64,768]{2,1,0:T(8,128)(2,1)S(1)}, bf16[2,64,768]{2,1,0:T(8,128)(2,1)S(1)}, u32[]{:S(2)}, u32[]{:S(2)}) %collective-permute-start.5) | collective-permute-done | bytes 196640 | tf_op jit(solution)/shard_map/ppermute | solution.py:37
  49.6 3.4 %collective-permute-done.6 = bf16[2,64,768]{2,1,0:T(8,128)(2,1)S(1)} collective-permute-done((bf16[2,64,768]{2,1,0:T(8,128)(2,1)S(1)}, bf16[2,64,768]{2,1,0:T(8,128)(2,1)S(1)}, u32[]{:S(2)}, u32[]{:S(2)}) %collective-permute-start.6) | collective-permute-done | bytes 196640 | tf_op jit(solution)/shard_map/ppermute | solution.py:37
  53.0 0.0 collective-permute-done.7
  53.0 0.0 copy-start
  53.0 1.9 %collective-permute-start.8 = (bf16[4,4,64,768]{3,2,1,0:T(8,128)(2,1)S(1)}, bf16[4,4,64,768]{3,2,1,0:T(8,128)(2,1)S(1)}, u32[]{:S(2)}, u32[]{:S(2)}) collective-permute-start(bf16[4,4,64,768]{3,2,1,0:T(8,128)(2,1)S(1)} %bitcast.12), channel_id=1, source_target_pairs={{0,8},{8,0},{1,9},{9,1},{2,10},{10,2},{3,11},{11,3},{4,12},{12,4},... | collective-permute-start | bytes 4718600 | tf_op jit(solution)/shard_map/ppermute | solution.py:37
  55.0 0.0 copy-done.5
  55.0 0.0 copy-done.6
  55.0 0.0 copy-start.2
  55.0 4.9 %collective-permute-start.1 = (bf16[256,256]{1,0:T(8,128)(2,1)S(1)}, bf16[256,256]{1,0:T(8,128)(2,1)S(1)}, u32[]{:S(2)}, u32[]{:S(2)}) collective-permute-start(bf16[256,256]{1,0:T(8,128)(2,1)S(1)} %constant_dynamic-update-slice_fusion.kv0_ref), channel_id=1, source_target_pairs={{0,16},{8,24},{16,32},{24,40},{32,48},{40,56},{48,64},{56,72},{64,... | collective-permute-start | bytes 393224 | tf_op jit(solution)/shard_map/ppermute | solution.py:32
  60.0 2.1 %collective-permute-start = (bf16[256,256]{1,0:T(8,128)(2,1)S(1)}, bf16[256,256]{1,0:T(8,128)(2,1)S(1)}, u32[]{:S(2)}, u32[]{:S(2)}) collective-permute-start(bf16[256,256]{1,0:T(8,128)(2,1)S(1)} %constant_dynamic-update-slice_fusion.kv0_ref), channel_id=1, source_target_pairs={{0,8},{8,16},{16,24},{24,32},{32,40},{40,48},{48,56},{56,64},{64,7... | collective-permute-start | bytes 393224 | tf_op jit(solution)/shard_map/ppermute | solution.py:32
  62.1 0.0 copy-done.7
  62.1 0.7 copy.11.picks_ref
  62.8 0.6 pad_add_fusion.where_ref
  63.4 0.0 collective-permute-done.1.kv2_ref
  63.4 0.0 copy-start.3
  63.4 0.0 collective-permute-done.kv1_ref
  63.4 0.0 copy-done.2
  63.5 0.6 copy-done.3
  64.1 0.0 copy-start.4
  64.1 0.7 copy-done.4
  64.7 5.3 %attention.1 = (bf16[256,512]{1,0:T(8,128)(2,1)}, f32[256,256]{1,0:T(8,128)}, bf16[256,256]{1,0:T(8,128)(2,1)}, bf16[256,256]{1,0:T(8,128)(2,1)}) custom-call(s32[3]{0:T(128)} %pad_add_fusion.where_ref, s32[2,4,3]{2,1,0:T(4,128)} %copy.11.picks_ref, bf16[256,512]{1,0:T(8,128)(2,1)} %q_ref.1, bf16[256,512]{1,0:T(8,128)(2,1)} %do_ref.1, ...), custom_call_target="tpu_custom_call" | custom-call | tf_op jit(solution)/shard_map/attention/pallas_call | solution.py:108
  70.0 1.3 collective-permute-start.2
  71.3 1.3 collective-permute-start.3
  72.6 16.9 %all-gather = bf16[512,512]{1,0:T(8,128)(2,1)} all-gather(bf16[256,512]{1,0:T(8,128)(2,1)} %get-tuple-element.9), channel_id=2, replica_groups=mesh['zh'=4,'zl'=4,'xh'=2,'core'=2,'xl'=2,'y'=4] {'xh'}, dimensions={0}, use_global_device_ids=true | all-gather | bytes 786432 | tf_op jit(solution)/shard_map/all_gather | solution.py:195
  89.5 0.0 collective-permute-done.2
  89.5 0.0 collective-permute-done.3
  89.5 1.0 add_convert_fusion
  90.5 8.2 %all-gather.1 = bf16[512,256]{1,0:T(8,128)(2,1)} all-gather(bf16[256,256]{1,0:T(8,128)(2,1)S(1)} %add_convert_fusion), channel_id=3, replica_groups=mesh['zh'=4,'zl'=4,'xh'=2,'core'=2,'xl'=2,'y'=4] {'xh'}, dimensions={0}, use_global_device_ids=true | all-gather | bytes 393216 | tf_op jit(solution)/shard_map/all_gather | solution.py:197
  98.7 0.0 copy-done
  98.7 0.0 collective-permute-done.8.wo_ref
  98.7 0.0 copy-start.1
  98.7 1.2 copy-done.1
  99.9 5.3 %project.1 = bf16[16,256,256]{2,1,0:T(8,128)(2,1)} custom-call(s32[3]{0:T(128)} %pad_add_fusion.where_ref, bf16[2,256,512]{2,1,0:T(8,128)(2,1)} %bitcast.14, bf16[2,256,256]{2,1,0:T(8,128)(2,1)} %bitcast.15, bf16[4,4,64,768]{3,2,1,0:T(8,128)(2,1)} %bitcast.13, bf16[4,4,64,768]{3,2,1,0:T(8,128)(2,1)} %copy-done.1), custom_call_target="tpu_custom_call" | custom-call | tf_op jit(solution)/shard_map/project/pallas_call | solution.py:142
  105.2 34.5 %all_to_all.5.in_ref = bf16[16,256,256]{2,1,0:T(8,128)(2,1)} all-to-all(bf16[16,256,256]{2,1,0:T(8,128)(2,1)} %project.1), channel_id=1, replica_groups=mesh['zh'=4,'zl'=4,'xh'=2,'core'=2,'xl'=2,'y'=4] {'xh','xl','y'}, dimensions={0} | all-to-all | bytes 4194304 | tf_op jit(solution)/shard_map/all_to_all | solution.py:201
  139.7 3.5 %total.1 = bf16[256,512]{1,0:T(8,128)(2,1)} custom-call(bf16[16,256,256]{2,1,0:T(8,128)(2,1)} %all_to_all.5.in_ref), custom_call_target="tpu_custom_call" | custom-call | tf_op jit(solution)/shard_map/total/pallas_call | solution.py:164
  (8 shorter events, 0.2 us)
Async XLA Ops:
  31.4 14.0 %collective-permute-start.4 = (bf16[4,64,768]{2,1,0:T(8,128)(2,1)S(1)}, bf16[4,64,768]{2,1,0:T(8,128)(2,1)S(1)}, u32[]{:S(2)}, u32[]{:S(2)}) collective-permute-start(bf16[4,64,768]{2,1,0:T(8,128)(2,1)S(1)} %bitcast.9), channel_id=1, source_target_pairs={{0,480},{32,0},{64,32},{96,64},{128,96},{160,128},{192,160},{224,1... | collective-permute-start | bytes 1179656 | tf_op jit(solution)/shard_map/ppermute | solution.py:37
  34.2 18.8 %collective-permute-start.7 = (bf16[4,64,768]{2,1,0:T(8,128)(2,1)S(1)}, bf16[4,64,768]{2,1,0:T(8,128)(2,1)S(1)}, u32[]{:S(2)}, u32[]{:S(2)}) collective-permute-start(bf16[4,64,768]{2,1,0:T(8,128)(2,1)S(1)} %bitcast.10), channel_id=1, source_target_pairs={{0,32},{32,64},{64,96},{96,128},{128,160},{160,192},{192,224},{224... | collective-permute-start | bytes 1179656 | tf_op jit(solution)/shard_map/ppermute | solution.py:37
  37.3 12.3 %collective-permute-start.5 = (bf16[2,64,768]{2,1,0:T(8,128)(2,1)S(1)}, bf16[2,64,768]{2,1,0:T(8,128)(2,1)S(1)}, u32[]{:S(2)}, u32[]{:S(2)}) collective-permute-start(bf16[2,64,768]{2,1,0:T(8,128)(2,1)S(1)} %bitcast.17), channel_id=1, source_target_pairs={{0,448},{32,480},{64,0},{96,32},{128,64},{160,96},{192,128},{224,1... | collective-permute-start | bytes 589832 | tf_op jit(solution)/shard_map/ppermute | solution.py:37
  40.7 14.3 %copy-start.5 = (bf16[256,128]{1,0:T(8,128)(2,1)S(1)}, bf16[256,128]{1,0:T(8,128)(2,1)}, u32[]{:S(2)}) copy-start(bf16[256,128]{1,0:T(8,128)(2,1)} %param.11) | copy-start | bytes 196612
  40.7 14.3 %copy-start.6 = (bf16[256,128]{1,0:T(8,128)(2,1)S(1)}, bf16[256,128]{1,0:T(8,128)(2,1)}, u32[]{:S(2)}) copy-start(bf16[256,128]{1,0:T(8,128)(2,1)} %param.12) | copy-start | bytes 196612
  40.7 21.4 %copy-start.7 = (s32[2,4,3]{1,0,2:T(2,128)S(1)}, s32[2,4,3]{1,0,2:T(2,128)}, u32[]{:S(2)}) copy-start(s32[2,4,3]{1,0,2:T(2,128)} %param.16) | copy-start | bytes 292
  40.7 12.3 %collective-permute-start.6 = (bf16[2,64,768]{2,1,0:T(8,128)(2,1)S(1)}, bf16[2,64,768]{2,1,0:T(8,128)(2,1)S(1)}, u32[]{:S(2)}, u32[]{:S(2)}) collective-permute-start(bf16[2,64,768]{2,1,0:T(8,128)(2,1)S(1)} %bitcast.16), channel_id=1, source_target_pairs={{0,64},{32,96},{64,128},{96,160},{128,192},{160,224},{192,256},{22... | collective-permute-start | bytes 589832 | tf_op jit(solution)/shard_map/ppermute | solution.py:37
  53.0 45.7 %copy-start = (bf16[16,64,768]{2,1,0:T(8,128)(2,1)}, bf16[16,64,768]{2,1,0:T(8,128)(2,1)S(1)}, u32[]{:S(2)}) copy-start(bf16[16,64,768]{2,1,0:T(8,128)(2,1)S(1)} %constant_dynamic-update-slice_fusion.2) | copy-start | bytes 4718596
  53.0 45.7 %collective-permute-start.8 = (bf16[4,4,64,768]{3,2,1,0:T(8,128)(2,1)S(1)}, bf16[4,4,64,768]{3,2,1,0:T(8,128)(2,1)S(1)}, u32[]{:S(2)}, u32[]{:S(2)}) collective-permute-start(bf16[4,4,64,768]{3,2,1,0:T(8,128)(2,1)S(1)} %bitcast.12), channel_id=1, source_target_pairs={{0,8},{8,0},{1,9},{9,1},{2,10},{10,2},{3,11},{11,3},{4,12},{12,4},... | collective-permute-start | bytes 4718600 | tf_op jit(solution)/shard_map/ppermute | solution.py:37
  55.0 8.4 %copy-start.2 = (bf16[256,256]{1,0:T(8,128)(2,1)}, bf16[256,256]{1,0:T(8,128)(2,1)S(1)}, u32[]{:S(2)}) copy-start(bf16[256,256]{1,0:T(8,128)(2,1)S(1)} %constant_dynamic-update-slice_fusion.kv0_ref) | copy-start | bytes 393220
  55.0 8.4 %collective-permute-start.1 = (bf16[256,256]{1,0:T(8,128)(2,1)S(1)}, bf16[256,256]{1,0:T(8,128)(2,1)S(1)}, u32[]{:S(2)}, u32[]{:S(2)}) collective-permute-start(bf16[256,256]{1,0:T(8,128)(2,1)S(1)} %constant_dynamic-update-slice_fusion.kv0_ref), channel_id=1, source_target_pairs={{0,16},{8,24},{16,32},{24,40},{32,48},{40,56},{48,64},{56,72},{64,... | collective-permute-start | bytes 393224 | tf_op jit(solution)/shard_map/ppermute | solution.py:32
  60.0 3.5 %collective-permute-start = (bf16[256,256]{1,0:T(8,128)(2,1)S(1)}, bf16[256,256]{1,0:T(8,128)(2,1)S(1)}, u32[]{:S(2)}, u32[]{:S(2)}) collective-permute-start(bf16[256,256]{1,0:T(8,128)(2,1)S(1)} %constant_dynamic-update-slice_fusion.kv0_ref), channel_id=1, source_target_pairs={{0,8},{8,16},{16,24},{24,32},{32,40},{40,48},{48,56},{56,64},{64,7... | collective-permute-start | bytes 393224 | tf_op jit(solution)/shard_map/ppermute | solution.py:32
  63.4 0.6 copy-start.3
  64.1 0.7 copy-start.4
  70.0 19.5 %collective-permute-start.2 = (bf16[256,256]{1,0:T(8,128)(2,1)}, bf16[256,256]{1,0:T(8,128)(2,1)S(1)}, u32[]{:S(2)}, u32[]{:S(2)}) collective-permute-start(bf16[256,256]{1,0:T(8,128)(2,1)} %get-tuple-element.11), channel_id=1, source_target_pairs={{8,0},{16,8},{24,16},{32,24},{40,32},{48,40},{56,48},{64,56},{72,6... | collective-permute-start | bytes 393224 | tf_op jit(solution)/shard_map/ppermute | solution.py:32
  71.3 18.3 %collective-permute-start.3 = (bf16[256,256]{1,0:T(8,128)(2,1)}, bf16[256,256]{1,0:T(8,128)(2,1)S(1)}, u32[]{:S(2)}, u32[]{:S(2)}) collective-permute-start(bf16[256,256]{1,0:T(8,128)(2,1)} %get-tuple-element.12), channel_id=1, source_target_pairs={{16,0},{24,8},{32,16},{40,24},{48,32},{56,40},{64,48},{72,56},{80,... | collective-permute-start | bytes 393224 | tf_op jit(solution)/shard_map/ppermute | solution.py:32
  98.7 1.2 copy-start.1

commit v2 on v1

--- a/solution.py
+++ b/solution.py
@@ -38,11 +38,11 @@
 
 
 def attention_kernel(
-    where_ref, picks_ref, q_ref, do_ref, o_ref, lse_ref, kv0_ref, kv1_ref, kv2_ref,
+    picks_ref, q_ref, do_ref, o_ref, lse_ref, kv0_ref, kv1_ref, kv2_ref,
     aq_ref, own_ref, ret1_ref, ret2_ref,
 ):
     scaling = 1.0 / math.sqrt(HD)
-    first = where_ref[0] * 2
+    first = lax.axis_index(CTX) * 2
     tables = (kv2_ref, kv2_ref, kv1_ref, kv1_ref, kv0_ref, kv0_ref)
     sums = (ret2_ref, ret2_ref, ret1_ref, ret1_ref, own_ref, own_ref)
     key_at = lax.broadcasted_iota(jnp.int32, (BLK, BLK), 0)
@@ -78,9 +78,9 @@
                     p = jnp.where(causal, p, 0.0)
                 else:
                     m = 3 - s
-                    used = picks_ref[b, h, 0] == m
+                    used = picks_ref[0, b, h] == m
                     for t in range(1, 3):
-                        used = used | (picks_ref[b, h, t] == m)
+                        used = used | (picks_ref[t, b, h] == m)
                     used = used & (first + b - 1 - m >= 0)
                     p = jnp.where(used, p, 0.0)
                 p_parts.append(p.astype(BF))
@@ -101,7 +101,7 @@
         sums[c][half, HD:] = dv[c].astype(sums[c].dtype)
 
 
-def attention(where, picks, q, do, o, lse, kv0, kv1, kv2):
+def attention(picks, q, do, o, lse, kv0, kv1, kv2):
     tokens = q.shape[0]
     vm = pl.BlockSpec(memory_space=pltpu.VMEM)
     sm = pl.BlockSpec(memory_space=pltpu.SMEM)
@@ -113,49 +113,56 @@
             jax.ShapeDtypeStruct((tokens, 2 * HD), BF),
             jax.ShapeDtypeStruct((tokens, 2 * HD), BF),
         ),
-        in_specs=[sm, sm] + [vm] * 7,
+        in_specs=[sm] + [vm] * 7,
         out_specs=(vm,) * 4,
         name="attention",
-    )(where, picks, q, do, o, lse, kv0, kv1, kv2)
-
-
-def project_kernel(where_ref, aq_ref, akv_ref, wc_ref, wo_ref, out_ref):
-    zl = where_ref[1]
-    core = where_ref[2]
-    for head in range(8):
-        zh = head // 2
-        wide = []
-        for e in range(2):
-            k = lax.rem(2 * (head % 2) + e + 4 - zl, 4)
-            mine = wc_ref[k, zh]
-            other = wo_ref[k, zh]
-            wide.append(jnp.where(core == 0, mine, other))
-            wide.append(jnp.where(core == 0, other, mine))
-        w = jnp.concatenate(wide, axis=0)
-        for r in range(2):
-            total = dot(aq_ref[r], w[:, : GROUP * HD], NT) + dot(akv_ref[r], w[:, GROUP * HD :], NT)
-            out_ref[8 * r + head] = total.astype(BF)
-
-
-def project(where, aq, akv, wc, wo):
-    vm = pl.BlockSpec(memory_space=pltpu.VMEM)
+    )(picks.transpose(2, 0, 1), q, do, o, lse, kv0, kv1, kv2)
+
+
+def project_kernel(zl_ref, a_ref, m0_ref, o0_ref, m1_ref, o1_ref, out_ref):
+    w = jnp.concatenate([r[0, 0] for r in (m0_ref, o0_ref, m1_ref, o1_ref)], axis=0)
+    for r in range(2):
+        out_ref[r, 0] = dot(a_ref[r], w, NT).astype(BF)
+
+
+def project(zl, a, wc, wo):
+    rows = wc.shape[2]
+
+    def rows_of(e):
+        def at(head, zl_ref):
+            return (lax.rem(2 * lax.rem(head, 2) + e + 4 - zl_ref[0], 4), lax.div(head, 2), 0, 0)
+
+        return pl.BlockSpec((1, 1, rows, wc.shape[3]), at)
+
+    def whole(x):
+        return pl.BlockSpec(x.shape, lambda head, zl_ref: (0, 0, 0))
+
     return pl.pallas_call(
         project_kernel,
-        out_shape=jax.ShapeDtypeStruct((16, aq.shape[1], 256), BF),
-        in_specs=[pl.BlockSpec(memory_space=pltpu.SMEM)] + [vm] * 4,
-        out_specs=vm,
+        grid_spec=pltpu.PrefetchScalarGridSpec(
+            num_scalar_prefetch=1,
+            grid=(8,),
+            in_specs=[whole(a), rows_of(0), rows_of(0), rows_of(1), rows_of(1)],
+            out_specs=pl.BlockSpec(
+                (2, 1, a.shape[1], 4 * rows), lambda head, zl_ref: (0, head, 0, 0)
+            ),
+        ),
+        out_shape=jax.ShapeDtypeStruct((2, 8, a.shape[1], 4 * rows), BF),
         name="project",
-    )(where, aq, akv, wc, wo)
+    )(zl, a, wc, wo, wc, wo)
 
 
 def total_kernel(in_ref, out_ref):
+    swapped = lax.axis_index("core") == 1
     for xh in range(2):
         total = in_ref[8 * xh].astype(F32)
         for h in range(1, 8):
             total = total + in_ref[8 * xh + h].astype(F32)
         for e in range(2):
             at = 256 * e + 128 * xh
-            out_ref[:, at : at + 128] = total[:, 128 * e : 128 * e + 128].astype(BF)
+            tile = total[:, 128 * e : 128 * e + 128]
+            tile = jnp.where(swapped, pltpu.roll(tile, 64, 1), tile)
+            out_ref[:, at : at + 128] = tile.astype(BF)
 
 
 def totalled(parts):
@@ -171,34 +178,51 @@
     )(parts)
 
 
+def prepare_kernel(k_ref, v_ref, qw_ref, kw_ref, vw_ref, kv_ref, w_ref):
+    kv_ref[:, :HD] = k_ref[...]
+    kv_ref[:, HD:] = v_ref[...]
+    w_ref[:, : GROUP * HD] = qw_ref[...]
+    w_ref[:, GROUP * HD : GROUP * HD + HD] = kw_ref[...]
+    w_ref[:, GROUP * HD + HD :] = vw_ref[...]
+
+
+def prepared(keys, values, qw, kw, vw):
+    vm = pl.BlockSpec(memory_space=pltpu.VMEM)
+    return pl.pallas_call(
+        prepare_kernel,
+        out_shape=(
+            jax.ShapeDtypeStruct((keys.shape[0], 2 * HD), BF),
+            jax.ShapeDtypeStruct((qw.shape[0], qw.shape[1] + 2 * HD), BF),
+        ),
+        in_specs=[vm] * 5,
+        out_specs=(vm, vm),
+        name="prepare",
+    )(keys, values, qw, kw, vw)
+
+
 def per_device(
     queries, key_rows, value_rows, attn_out, out_grad, log_sums, block_picks,
     query_weight, key_weight, value_weight,
 ):
-    where = jnp.stack(
-        [lax.axis_index(CTX), lax.axis_index("zl"), lax.axis_index("core")]
-    ).astype(jnp.int32)
-    kv0 = jnp.concatenate([key_rows, value_rows], axis=1)
+    kv0, weight = prepared(key_rows, value_rows, query_weight, key_weight, value_weight)
     kv1 = passed_along(kv0, CTX, 1)
     kv2 = passed_along(kv0, CTX, 2)
-    weight = jnp.concatenate([query_weight, key_weight, value_weight], axis=1)
     w0 = lax.all_gather(weight, "zh")
     w1 = shifted(w0, Z, -1)
     w3 = shifted(w0, Z, 1)
-    w2a = shifted(w0[:2], Z, -2)
-    w2b = shifted(w0[2:], Z, 2)
+    w2 = lax.ppermute(w0, Z, [((z + 2 if z % 2 == 0 else z - 2) % 16, z) for z in range(16)])
     aq, own, ret1, ret2 = attention(
-        where, block_picks, queries, out_grad, attn_out, log_sums, kv0, kv1, kv2
+        block_picks, queries, out_grad, attn_out, log_sums, kv0, kv1, kv2
     )
     back1 = passed_along(ret1, CTX, -1)
     back2 = passed_along(ret2, CTX, -2)
-    aq_all = lax.all_gather(aq, "xh")
+    wc = jnp.stack([w0, w1, w2, w3])
+    wo = shifted(wc, "core", 1)
     akv = (own + back1.astype(F32) + back2.astype(F32)).astype(BF)
-    akv_all = lax.all_gather(akv, "xh")
-    wc = jnp.concatenate([w0, w1, w2a, w2b, w3], axis=0).reshape(4, 4, *weight.shape)
-    wo = shifted(wc, "core", 1)
-    parts = project(where, aq_all, akv_all, wc, wo)
-    parts = lax.all_to_all(parts, ("xh", "xl", "y"), 0, 0)
+    a_all = lax.all_gather(jnp.concatenate([aq, akv], axis=1), "xh")
+    zl = lax.axis_index("zl").reshape(1).astype(jnp.int32)
+    parts = project(zl, a_all, wc, wo)
+    parts = lax.all_to_all(parts.reshape(16, *parts.shape[2:]), ("xh", "xl", "y"), 0, 0)
     return totalled(parts)
 
 

time: 144 us -> 145 us (level)
  the two profiles are of different devices: /device:TPU:8 before, /device:TPU:32 now
where the time goes in v2:
time: 145 us; the launch traced here: 144 us
  blocking collectives  75.4 us (52%)
  waiting for transfers between devices  23.3 us (16%)
  starting transfers between devices  23.1 us (16%)
  Pallas kernels  18.3 us (13%)
  other arithmetic  2.17 us (1%)
  local copies, waits for them, and re-layouts  1.83 us (1%)
    all_to_all x1, blocking collectives, per_device(): lax.all_to_all(parts.reshape(16, *parts.shape[2:]), ('xh', 'xl', 'y'), 0, 0)  33 us
    all_gather x1, blocking collectives, per_device(): w0 = lax.all_gather(weight, 'zh')  29.4 us
    ppermute x4, waiting for transfers between devices, passed_along(): return lax.ppermute(x, axis, pairs)  13.3 us
    all_gather x1, blocking collectives, per_device(): a_all = lax.all_gather(jnp.concatenate([aq, akv], axis=1), 'xh')  12.9 us
    ppermute x4, starting transfers between devices, passed_along(): return lax.ppermute(x, axis, pairs)  11.7 us
    pallas_call x1, Pallas kernels, project(): pl.pallas_call(project_kernel, grid_spec=pltpu.PrefetchScalarGridSpec(num...  7.79 us
    ppermute x3, starting transfers between devices, shifted(): return lax.ppermute(x, axis, [(i, (i + by) % n) for i in range(n)])  7.76 us
    pallas_call x1, Pallas kernels, attention(): pl.pallas_call(attention_kernel, out_shape=(jax.ShapeDtypeStruct(q.shape,...  5.26 us
  transfers between devices with their start and end apart: 8, of which 6 were waited for; matrix products, arithmetic and copies ran while one was open for 1% of the time, Pallas kernels for 4%

profile of v2, /device:TPU:32, one launch (start us, length us, event | category | flops | bytes accessed | tf_op | source)
XLA Modules:
  0.0 144.2 jit_solution(883991838925595563)
XLA Ops:
  0.0 1.6 %prepare.1 = (bf16[256,256]{1,0:T(8,128)(2,1)}, bf16[64,768]{1,0:T(8,128)(2,1)}) custom-call(bf16[256,128]{1,0:T(8,128)(2,1)} %k_ref.1, bf16[256,128]{1,0:T(8,128)(2,1)} %v_ref.1, bf16[64,512]{1,0:T(8,128)(2,1)} %qw_ref.1, bf16[64,128]{1,0:T(8,128)(2,1)} %kw_ref.1, bf16[64,128]{1,0:T(8,128)(2,1)} %vw_ref.1), custom_call_target="tpu_custom_call" | custom-call | tf_op jit(solution)/shard_map/prepare/pallas_call | solution.py:191
  1.6 29.4 %all-gather.1 = bf16[256,768]{1,0:T(8,128)(2,1)S(1)} all-gather(bf16[64,768]{1,0:T(8,128)(2,1)} %get-tuple-element.16), channel_id=3, replica_groups=mesh['zh'=4,'zl'=4,'xh'=2,'core'=2,'xl'=2,'y'=4] {'zh'}, dimensions={0}, use_global_device_ids=true | all-gather | bytes 491520 | tf_op jit(solution)/shard_map/all_gather | solution.py:210
  31.1 3.5 %collective-permute-start.5 = (bf16[4,64,768]{2,1,0:T(8,128)(2,1)S(1)}, bf16[4,64,768]{2,1,0:T(8,128)(2,1)S(1)}, u32[]{:S(2)}, u32[]{:S(2)}) collective-permute-start(bf16[4,64,768]{2,1,0:T(8,128)(2,1)S(1)} %bitcast.11), channel_id=1, source_target_pairs={{64,0},{480,32},{128,64},{32,96},{192,128},{96,160},{256,192},{160... | collective-permute-start | bytes 1179656 | tf_op jit(solution)/shard_map/ppermute | solution.py:213
  34.6 3.1 %collective-permute-start.4 = (bf16[4,64,768]{2,1,0:T(8,128)(2,1)S(1)}, bf16[4,64,768]{2,1,0:T(8,128)(2,1)S(1)}, u32[]{:S(2)}, u32[]{:S(2)}) collective-permute-start(bf16[4,64,768]{2,1,0:T(8,128)(2,1)S(1)} %bitcast.12), channel_id=1, source_target_pairs={{0,480},{32,0},{64,32},{96,64},{128,96},{160,128},{192,160},{224,1... | collective-permute-start | bytes 1179656 | tf_op jit(solution)/shard_map/ppermute | solution.py:37
  37.7 2.7 %collective-permute-start.6 = (bf16[4,64,768]{2,1,0:T(8,128)(2,1)S(1)}, bf16[4,64,768]{2,1,0:T(8,128)(2,1)S(1)}, u32[]{:S(2)}, u32[]{:S(2)}) collective-permute-start(bf16[4,64,768]{2,1,0:T(8,128)(2,1)S(1)} %bitcast.13), channel_id=1, source_target_pairs={{0,32},{32,64},{64,96},{96,128},{128,160},{160,192},{192,224},{224... | collective-permute-start | bytes 1179656 | tf_op jit(solution)/shard_map/ppermute | solution.py:37
  40.5 5.0 %collective-permute-done.5 = bf16[4,64,768]{2,1,0:T(8,128)(2,1)S(1)} collective-permute-done((bf16[4,64,768]{2,1,0:T(8,128)(2,1)S(1)}, bf16[4,64,768]{2,1,0:T(8,128)(2,1)S(1)}, u32[]{:S(2)}, u32[]{:S(2)}) %collective-permute-start.5) | collective-permute-done | bytes 393248 | tf_op jit(solution)/shard_map/ppermute | solution.py:213
  45.5 4.0 %collective-permute-done.4 = bf16[4,64,768]{2,1,0:T(8,128)(2,1)S(1)} collective-permute-done((bf16[4,64,768]{2,1,0:T(8,128)(2,1)S(1)}, bf16[4,64,768]{2,1,0:T(8,128)(2,1)S(1)}, u32[]{:S(2)}, u32[]{:S(2)}) %collective-permute-start.4) | collective-permute-done | bytes 393248 | tf_op jit(solution)/shard_map/ppermute | solution.py:37
  49.6 0.9 collective-permute-done.6
  50.5 0.0 copy-start.2
  50.5 0.2 pad_maximum_fusion.m0_ref.m1_ref
  50.7 0.0 copy-start
  50.7 1.9 %collective-permute-start.7 = (bf16[4,4,64,768]{3,2,1,0:T(8,128)(2,1)S(1)}, bf16[4,4,64,768]{3,2,1,0:T(8,128)(2,1)S(1)}, u32[]{:S(2)}, u32[]{:S(2)}) collective-permute-start(bf16[4,4,64,768]{3,2,1,0:T(8,128)(2,1)S(1)} %pad_maximum_fusion.m0_ref.m1_ref), channel_id=1, source_target_pairs={{0,8},{8,0},{1,9},{9,1},{2,10},{10,2},{3,11},{11,3},{4,12},{12,4},... | collective-permute-start | bytes 4718600 | tf_op jit(solution)/shard_map/ppermute | solution.py:37
  52.6 0.0 copy-done.2
  52.6 4.9 %collective-permute-start.1 = (bf16[256,256]{1,0:T(8,128)(2,1)S(1)}, bf16[256,256]{1,0:T(8,128)(2,1)S(1)}, u32[]{:S(2)}, u32[]{:S(2)}) collective-permute-start(bf16[256,256]{1,0:T(8,128)(2,1)S(1)} %copy-done.2), channel_id=1, source_target_pairs={{0,16},{8,24},{16,32},{24,40},{32,48},{40,56},{48,64},{56,72},{64,... | collective-permute-start | bytes 393224 | tf_op jit(solution)/shard_map/ppermute | solution.py:32
  57.6 2.1 %collective-permute-start = (bf16[256,256]{1,0:T(8,128)(2,1)S(1)}, bf16[256,256]{1,0:T(8,128)(2,1)S(1)}, u32[]{:S(2)}, u32[]{:S(2)}) collective-permute-start(bf16[256,256]{1,0:T(8,128)(2,1)S(1)} %copy-done.2), channel_id=1, source_target_pairs={{0,8},{8,16},{16,24},{24,32},{32,40},{40,48},{48,56},{56,64},{64,7... | collective-permute-start | bytes 393224 | tf_op jit(solution)/shard_map/ppermute | solution.py:32
  59.7 3.1 %collective-permute-done.1.kv2_ref = bf16[256,256]{1,0:T(8,128)(2,1)S(1)} collective-permute-done((bf16[256,256]{1,0:T(8,128)(2,1)S(1)}, bf16[256,256]{1,0:T(8,128)(2,1)S(1)}, u32[]{:S(2)}, u32[]{:S(2)}) %collective-permute-start.1) | collective-permute-done | bytes 131104 | tf_op jit(solution)/shard_map/ppermute | solution.py:32
  62.8 0.0 copy-start.3
  62.8 3.4 %collective-permute-done.kv1_ref = bf16[256,256]{1,0:T(8,128)(2,1)S(1)} collective-permute-done((bf16[256,256]{1,0:T(8,128)(2,1)S(1)}, bf16[256,256]{1,0:T(8,128)(2,1)S(1)}, u32[]{:S(2)}, u32[]{:S(2)}) %collective-permute-start) | collective-permute-done | bytes 131104 | tf_op jit(solution)/shard_map/ppermute | solution.py:32
  66.3 0.0 copy-start.4
  66.3 0.0 copy-done.3
  66.3 0.7 copy-done.4
  66.9 5.3 %attention.1 = (bf16[256,512]{1,0:T(8,128)(2,1)}, f32[256,256]{1,0:T(8,128)}, bf16[256,256]{1,0:T(8,128)(2,1)}, bf16[256,256]{1,0:T(8,128)(2,1)}) custom-call(s32[3,2,4]{2,1,0:T(2,128)} %bitcast.18, bf16[256,512]{1,0:T(8,128)(2,1)} %q_ref.1, bf16[256,512]{1,0:T(8,128)(2,1)} %do_ref.1, bf16[256,512]{1,0:T(8,128)(2,1)} %o_ref.1, f32[4,256]{1,0:T(4,128)} %lse_ref.1, ...), custom_call_target="tpu_custom_call" | custom-call | tf_op jit(solution)/shard_map/attention/pallas_call | solution.py:108
  72.2 1.9 %collective-permute-start.2 = (bf16[256,256]{1,0:T(8,128)(2,1)}, bf16[256,256]{1,0:T(8,128)(2,1)S(1)}, u32[]{:S(2)}, u32[]{:S(2)}) collective-permute-start(bf16[256,256]{1,0:T(8,128)(2,1)} %get-tuple-element.14), channel_id=1, source_target_pairs={{8,0},{16,8},{24,16},{32,24},{40,32},{48,40},{56,48},{64,56},{72,6... | collective-permute-start | bytes 393224 | tf_op jit(solution)/shard_map/ppermute | solution.py:32
  74.1 2.8 %collective-permute-start.3 = (bf16[256,256]{1,0:T(8,128)(2,1)}, bf16[256,256]{1,0:T(8,128)(2,1)S(1)}, u32[]{:S(2)}, u32[]{:S(2)}) collective-permute-start(bf16[256,256]{1,0:T(8,128)(2,1)} %get-tuple-element.15), channel_id=1, source_target_pairs={{16,0},{24,8},{32,16},{40,24},{48,32},{56,40},{64,48},{72,56},{80,... | collective-permute-start | bytes 393224 | tf_op jit(solution)/shard_map/ppermute | solution.py:32
  76.9 0.0 collective-permute-done.2
  76.9 6.7 %collective-permute-done.3 = bf16[256,256]{1,0:T(8,128)(2,1)S(1)} collective-permute-done((bf16[256,256]{1,0:T(8,128)(2,1)}, bf16[256,256]{1,0:T(8,128)(2,1)S(1)}, u32[]{:S(2)}, u32[]{:S(2)}) %collective-permute-start.3) | collective-permute-done | bytes 131104 | tf_op jit(solution)/shard_map/ppermute | solution.py:32
  83.6 1.0 add_convert_fusion
  84.6 1.0 pad_maximum_fusion.1
  85.6 12.9 %all-gather = bf16[512,768]{1,0:T(8,128)(2,1)} all-gather(bf16[256,768]{1,0:T(8,128)(2,1)S(1)} %pad_maximum_fusion.1), channel_id=2, replica_groups=mesh['zh'=4,'zl'=4,'xh'=2,'core'=2,'xl'=2,'y'=4] {'xh'}, dimensions={0}, use_global_device_ids=true | all-gather | bytes 1179648 | tf_op jit(solution)/shard_map/all_gather | solution.py:222
  98.5 0.0 copy-done
  98.5 0.0 collective-permute-done.7.o0_ref.o1_ref
  98.5 0.0 copy-start.1
  98.5 1.2 copy-done.1
  99.7 7.8 %project.1 = bf16[2,8,256,256]{3,2,1,0:T(8,128)(2,1)} custom-call(s32[1]{0:T(128)} %bitcast.zl_ref, bf16[2,256,768]{2,1,0:T(8,128)(2,1)} %bitcast.10, bf16[4,4,64,768]{3,2,1,0:T(8,128)(2,1)} %copy-done, bf16[4,4,64,768]{3,2,1,0:T(8,128)(2,1)} %copy-done.1, bf16[4,4,64,768]{3,2,1,0:T(8,128)(2,1)} %copy-done, bf16[4,4,64,768]{3,2,1,0:T(8,128)(2,1)} %copy-done.1), custom_call_target="tpu_custom_call" | custom-call | tf_op jit(solution)/shard_map/project/pallas_call | solution.py:140
  107.5 33.0 %all_to_all.5.in_ref = bf16[16,256,256]{2,1,0:T(8,128)(2,1)} all-to-all(bf16[16,256,256]{2,1,0:T(8,128)(2,1)} %bitcast.9), channel_id=1, replica_groups=mesh['zh'=4,'zl'=4,'xh'=2,'core'=2,'xl'=2,'y'=4] {'xh','xl','y'}, dimensions={0} | all-to-all | bytes 4194304 | tf_op jit(solution)/shard_map/all_to_all | solution.py:225
  140.5 3.7 %total.1 = bf16[256,512]{1,0:T(8,128)(2,1)} custom-call(bf16[16,256,256]{2,1,0:T(8,128)(2,1)} %all_to_all.5.in_ref), custom_call_target="tpu_custom_call" | custom-call | tf_op jit(solution)/shard_map/total/pallas_call | solution.py:171
Async XLA Ops:
  31.1 14.5 %collective-permute-start.5 = (bf16[4,64,768]{2,1,0:T(8,128)(2,1)S(1)}, bf16[4,64,768]{2,1,0:T(8,128)(2,1)S(1)}, u32[]{:S(2)}, u32[]{:S(2)}) collective-permute-start(bf16[4,64,768]{2,1,0:T(8,128)(2,1)S(1)} %bitcast.11), channel_id=1, source_target_pairs={{64,0},{480,32},{128,64},{32,96},{192,128},{96,160},{256,192},{160... | collective-permute-start | bytes 1179656 | tf_op jit(solution)/shard_map/ppermute | solution.py:213
  34.6 14.9 %collective-permute-start.4 = (bf16[4,64,768]{2,1,0:T(8,128)(2,1)S(1)}, bf16[4,64,768]{2,1,0:T(8,128)(2,1)S(1)}, u32[]{:S(2)}, u32[]{:S(2)}) collective-permute-start(bf16[4,64,768]{2,1,0:T(8,128)(2,1)S(1)} %bitcast.12), channel_id=1, source_target_pairs={{0,480},{32,0},{64,32},{96,64},{128,96},{160,128},{192,160},{224,1... | collective-permute-start | bytes 1179656 | tf_op jit(solution)/shard_map/ppermute | solution.py:37
  37.7 12.8 %collective-permute-start.6 = (bf16[4,64,768]{2,1,0:T(8,128)(2,1)S(1)}, bf16[4,64,768]{2,1,0:T(8,128)(2,1)S(1)}, u32[]{:S(2)}, u32[]{:S(2)}) collective-permute-start(bf16[4,64,768]{2,1,0:T(8,128)(2,1)S(1)} %bitcast.13), channel_id=1, source_target_pairs={{0,32},{32,64},{64,96},{96,128},{128,160},{160,192},{192,224},{224... | collective-permute-start | bytes 1179656 | tf_op jit(solution)/shard_map/ppermute | solution.py:37
  50.5 2.1 %copy-start.2 = (bf16[256,256]{1,0:T(8,128)(2,1)S(1)}, bf16[256,256]{1,0:T(8,128)(2,1)}, u32[]{:S(2)}) copy-start(bf16[256,256]{1,0:T(8,128)(2,1)} %get-tuple-element.11.kv0_ref) | copy-start | bytes 393220
  50.7 47.8 %copy-start = (bf16[4,4,64,768]{3,2,1,0:T(8,128)(2,1)}, bf16[4,4,64,768]{3,2,1,0:T(8,128)(2,1)S(1)}, u32[]{:S(2)}) copy-start(bf16[4,4,64,768]{3,2,1,0:T(8,128)(2,1)S(1)} %pad_maximum_fusion.m0_ref.m1_ref) | copy-start | bytes 4718596
  50.7 47.8 %collective-permute-start.7 = (bf16[4,4,64,768]{3,2,1,0:T(8,128)(2,1)S(1)}, bf16[4,4,64,768]{3,2,1,0:T(8,128)(2,1)S(1)}, u32[]{:S(2)}, u32[]{:S(2)}) collective-permute-start(bf16[4,4,64,768]{3,2,1,0:T(8,128)(2,1)S(1)} %pad_maximum_fusion.m0_ref.m1_ref), channel_id=1, source_target_pairs={{0,8},{8,0},{1,9},{9,1},{2,10},{10,2},{3,11},{11,3},{4,12},{12,4},... | collective-permute-start | bytes 4718600 | tf_op jit(solution)/shard_map/ppermute | solution.py:37
  52.6 10.2 %collective-permute-start.1 = (bf16[256,256]{1,0:T(8,128)(2,1)S(1)}, bf16[256,256]{1,0:T(8,128)(2,1)S(1)}, u32[]{:S(2)}, u32[]{:S(2)}) collective-permute-start(bf16[256,256]{1,0:T(8,128)(2,1)S(1)} %copy-done.2), channel_id=1, source_target_pairs={{0,16},{8,24},{16,32},{24,40},{32,48},{40,56},{48,64},{56,72},{64,... | collective-permute-start | bytes 393224 | tf_op jit(solution)/shard_map/ppermute | solution.py:32
  57.6 8.7 %collective-permute-start = (bf16[256,256]{1,0:T(8,128)(2,1)S(1)}, bf16[256,256]{1,0:T(8,128)(2,1)S(1)}, u32[]{:S(2)}, u32[]{:S(2)}) collective-permute-start(bf16[256,256]{1,0:T(8,128)(2,1)S(1)} %copy-done.2), channel_id=1, source_target_pairs={{0,8},{8,16},{16,24},{24,32},{32,40},{40,48},{48,56},{56,64},{64,7... | collective-permute-start | bytes 393224 | tf_op jit(solution)/shard_map/ppermute | solution.py:32
  62.8 3.4 %copy-start.3 = (bf16[256,256]{1,0:T(8,128)(2,1)}, bf16[256,256]{1,0:T(8,128)(2,1)S(1)}, u32[]{:S(2)}) copy-start(bf16[256,256]{1,0:T(8,128)(2,1)S(1)} %collective-permute-done.1.kv2_ref) | copy-start | bytes 393220
  66.3 0.7 copy-start.4
  72.2 4.7 %collective-permute-start.2 = (bf16[256,256]{1,0:T(8,128)(2,1)}, bf16[256,256]{1,0:T(8,128)(2,1)S(1)}, u32[]{:S(2)}, u32[]{:S(2)}) collective-permute-start(bf16[256,256]{1,0:T(8,128)(2,1)} %get-tuple-element.14), channel_id=1, source_target_pairs={{8,0},{16,8},{24,16},{32,24},{40,32},{48,40},{56,48},{64,56},{72,6... | collective-permute-start | bytes 393224 | tf_op jit(solution)/shard_map/ppermute | solution.py:32
  74.1 9.5 %collective-permute-start.3 = (bf16[256,256]{1,0:T(8,128)(2,1)}, bf16[256,256]{1,0:T(8,128)(2,1)S(1)}, u32[]{:S(2)}, u32[]{:S(2)}) collective-permute-start(bf16[256,256]{1,0:T(8,128)(2,1)} %get-tuple-element.15), channel_id=1, source_target_pairs={{16,0},{24,8},{32,16},{40,24},{48,32},{56,40},{64,48},{72,56},{80,... | collective-permute-start | bytes 393224 | tf_op jit(solution)/shard_map/ppermute | solution.py:32
  98.5 1.2 copy-start.1

commit v3 on v2

--- a/solution.py
+++ b/solution.py
@@ -116,40 +116,67 @@
         in_specs=[sm] + [vm] * 7,
         out_specs=(vm,) * 4,
         name="attention",
-    )(picks.transpose(2, 0, 1), q, do, o, lse, kv0, kv1, kv2)
-
-
-def project_kernel(zl_ref, a_ref, m0_ref, o0_ref, m1_ref, o1_ref, out_ref):
-    w = jnp.concatenate([r[0, 0] for r in (m0_ref, o0_ref, m1_ref, o1_ref)], axis=0)
-    for r in range(2):
-        out_ref[r, 0] = dot(a_ref[r], w, NT).astype(BF)
-
-
-def project(zl, a, wc, wo):
-    rows = wc.shape[2]
-
-    def rows_of(e):
-        def at(head, zl_ref):
-            return (lax.rem(2 * lax.rem(head, 2) + e + 4 - zl_ref[0], 4), lax.div(head, 2), 0, 0)
-
-        return pl.BlockSpec((1, 1, rows, wc.shape[3]), at)
-
-    def whole(x):
-        return pl.BlockSpec(x.shape, lambda head, zl_ref: (0, 0, 0))
-
+    )(
+        picks.transpose(2, 0, 1), q, do, o, lse, kv0,
+        placed_in(kv1, pltpu.VMEM), placed_in(kv2, pltpu.VMEM),
+    )
+
+
+def project_kernel(a_hbm, own_hbm, other_ref, out_hbm, a_ref, w_ref, out_ref, a_sem, w_sem, out_sem):
+    zl = lax.axis_index("zl")
+    load_a = pltpu.make_async_copy(a_hbm, a_ref, a_sem)
+    load_a.start()
+    loads = []
+    for head in range(8):
+        for e in range(2):
+            k = lax.rem(2 * (head % 2) + e + 4 - zl, 4)
+            loads.append(
+                pltpu.make_async_copy(
+                    own_hbm.at[k, head // 2], w_ref.at[head, e], w_sem.at[head, e]
+                )
+            )
+            loads[-1].start()
+    load_a.wait()
+    stores = []
+    for head in range(8):
+        wide = []
+        for e in range(2):
+            loads[2 * head + e].wait()
+            k = lax.rem(2 * (head % 2) + e + 4 - zl, 4)
+            wide += [w_ref[head, e], other_ref[k, head // 2]]
+        part = dot(a_ref[...], jnp.concatenate(wide, axis=0), NT).astype(BF)
+        for r in range(2):
+            at = 8 * r + head
+            out_ref[at] = part[256 * r : 256 * r + 256]
+            stores.append(pltpu.make_async_copy(out_ref.at[at], out_hbm.at[at], out_sem.at[at]))
+            stores[-1].start()
+    for store in stores:
+        store.wait()
+
+
+def placed_in(x, space):
+    return pltpu.with_memory_space_constraint(x, space)
+
+
+def project(a, wc, wo):
+    hbm = pl.BlockSpec(memory_space=pltpu.HBM)
+    rows, cols = wc.shape[2:]
+    a = a.reshape(-1, a.shape[2])
     return pl.pallas_call(
         project_kernel,
-        grid_spec=pltpu.PrefetchScalarGridSpec(
-            num_scalar_prefetch=1,
-            grid=(8,),
-            in_specs=[whole(a), rows_of(0), rows_of(0), rows_of(1), rows_of(1)],
-            out_specs=pl.BlockSpec(
-                (2, 1, a.shape[1], 4 * rows), lambda head, zl_ref: (0, head, 0, 0)
-            ),
-        ),
-        out_shape=jax.ShapeDtypeStruct((2, 8, a.shape[1], 4 * rows), BF),
+        out_shape=jax.ShapeDtypeStruct((16, 256, 4 * rows), BF),
+        in_specs=[hbm, hbm, pl.BlockSpec(memory_space=pltpu.VMEM)],
+        out_specs=hbm,
+        scratch_shapes=[
+            pltpu.VMEM(a.shape, BF),
+            pltpu.VMEM((8, 2, rows, cols), BF),
+            pltpu.VMEM((16, 256, 4 * rows), BF),
+            pltpu.SemaphoreType.DMA,
+            pltpu.SemaphoreType.DMA((8, 2)),
+            pltpu.SemaphoreType.DMA((16,)),
+        ],
         name="project",
-    )(zl, a, wc, wo, wc, wo)
+    )(a, wc, placed_in(wo, pltpu.VMEM))
 
 
 def total_kernel(in_ref, out_ref):
@@ -166,16 +193,14 @@
 
 
 def totalled(parts):
-    rows = parts.shape[1]
-    step = 64
+    vm = pl.BlockSpec(memory_space=pltpu.VMEM)
     return pl.pallas_call(
         total_kernel,
-        grid=(rows // step,),
-        out_shape=jax.ShapeDtypeStruct((rows, 512), BF),
-        in_specs=[pl.BlockSpec((16, step, 256), lambda i: (0, i, 0))],
-        out_specs=pl.BlockSpec((step, 512), lambda i: (i, 0)),
+        out_shape=jax.ShapeDtypeStruct((parts.shape[1], 512), BF),
+        in_specs=[vm],
+        out_specs=vm,
         name="total",
-    )(parts)
+    )(placed_in(parts, pltpu.VMEM))
 
 
 def prepare_kernel(k_ref, v_ref, qw_ref, kw_ref, vw_ref, kv_ref, w_ref):
@@ -220,9 +245,8 @@
     wo = shifted(wc, "core", 1)
     akv = (own + back1.astype(F32) + back2.astype(F32)).astype(BF)
     a_all = lax.all_gather(jnp.concatenate([aq, akv], axis=1), "xh")
-    zl = lax.axis_index("zl").reshape(1).astype(jnp.int32)
-    parts = project(zl, a_all, wc, wo)
-    parts = lax.all_to_all(parts.reshape(16, *parts.shape[2:]), ("xh", "xl", "y"), 0, 0)
+    parts = project(a_all, wc, wo)
+    parts = lax.all_to_all(parts, ("xh", "xl", "y"), 0, 0)
     return totalled(parts)
 
 

time: 145 us -> 140 us (0.966)
  Pallas kernels: 18.3 us -> 15.2 us
  local copies, waits for them, and re-layouts: 1.83 us -> 0.01 us
    pallas_call x2, Pallas kernels: 11.5 us -> 8.47 us  [the longest x1 7.42 us: project(): pl.pallas_call(project_kernel, out_shape=jax.ShapeDtypeStruct((16, 256, 4...]
    unnamed x10 -> x4, local copies, waits for them, and re-layouts: 1.83 us -> 0.01 us
where the time goes in v3:
time: 140 us; the launch traced here: 139 us
  blocking collectives  75.3 us (54%)
  waiting for transfers between devices  23.3 us (17%)
  starting transfers between devices  23.1 us (16%)
  Pallas kernels  15.2 us (11%)
  other arithmetic  2.18 us (2%)
    all_to_all x1, blocking collectives, per_device(): parts = lax.all_to_all(parts, ('xh', 'xl', 'y'), 0, 0)  33 us
    all_gather x1, blocking collectives, per_device(): w0 = lax.all_gather(weight, 'zh')  29.4 us
    ppermute x4, waiting for transfers between devices, passed_along(): return lax.ppermute(x, axis, pairs)  13.3 us
    all_gather x1, blocking collectives, per_device(): a_all = lax.all_gather(jnp.concatenate([aq, akv], axis=1), 'xh')  12.9 us
    ppermute x4, starting transfers between devices, passed_along(): return lax.ppermute(x, axis, pairs)  11.7 us
    ppermute x3, starting transfers between devices, shifted(): return lax.ppermute(x, axis, [(i, (i + by) % n) for i in range(n)])  7.76 us
    pallas_call x1, Pallas kernels, project(): pl.pallas_call(project_kernel, out_shape=jax.ShapeDtypeStruct((16, 256, 4...  7.42 us
    pallas_call x1, Pallas kernels, attention(): pl.pallas_call(attention_kernel, out_shape=(jax.ShapeDtypeStruct(q.shape,...  5.15 us
  transfers between devices with their start and end apart: 8, of which 6 were waited for; matrix products, arithmetic and copies ran while one was open for 1% of the time, Pallas kernels for 4%

profile of v3, /device:TPU:32, one launch (start us, length us, event | category | flops | bytes accessed | tf_op | source)
XLA Modules:
  0.0 139.2 jit_solution(17408288790768405069)
XLA Ops:
  0.0 1.6 %prepare.1 = (bf16[256,256]{1,0:T(8,128)(2,1)}, bf16[64,768]{1,0:T(8,128)(2,1)}) custom-call(bf16[256,128]{1,0:T(8,128)(2,1)} %k_ref.1, bf16[256,128]{1,0:T(8,128)(2,1)} %v_ref.1, bf16[64,512]{1,0:T(8,128)(2,1)} %qw_ref.1, bf16[64,128]{1,0:T(8,128)(2,1)} %kw_ref.1, bf16[64,128]{1,0:T(8,128)(2,1)} %vw_ref.1), custom_call_target="tpu_custom_call" | custom-call | tf_op jit(solution)/shard_map/prepare/pallas_call | solution.py:216
  1.6 29.4 %all-gather.1 = bf16[256,768]{1,0:T(8,128)(2,1)S(1)} all-gather(bf16[64,768]{1,0:T(8,128)(2,1)} %get-tuple-element.16), channel_id=3, replica_groups=mesh['zh'=4,'zl'=4,'xh'=2,'core'=2,'xl'=2,'y'=4] {'zh'}, dimensions={0}, use_global_device_ids=true | all-gather | bytes 491520 | tf_op jit(solution)/shard_map/all_gather | solution.py:235
  31.1 3.5 %collective-permute-start.5 = (bf16[4,64,768]{2,1,0:T(8,128)(2,1)S(1)}, bf16[4,64,768]{2,1,0:T(8,128)(2,1)S(1)}, u32[]{:S(2)}, u32[]{:S(2)}) collective-permute-start(bf16[4,64,768]{2,1,0:T(8,128)(2,1)S(1)} %bitcast.6), channel_id=1, source_target_pairs={{64,0},{480,32},{128,64},{32,96},{192,128},{96,160},{256,192},{160... | collective-permute-start | bytes 1179656 | tf_op jit(solution)/shard_map/ppermute | solution.py:238
  34.6 3.1 %collective-permute-start.4 = (bf16[4,64,768]{2,1,0:T(8,128)(2,1)S(1)}, bf16[4,64,768]{2,1,0:T(8,128)(2,1)S(1)}, u32[]{:S(2)}, u32[]{:S(2)}) collective-permute-start(bf16[4,64,768]{2,1,0:T(8,128)(2,1)S(1)} %bitcast.7), channel_id=1, source_target_pairs={{0,480},{32,0},{64,32},{96,64},{128,96},{160,128},{192,160},{224,1... | collective-permute-start | bytes 1179656 | tf_op jit(solution)/shard_map/ppermute | solution.py:37
  37.7 2.7 %collective-permute-start.6 = (bf16[4,64,768]{2,1,0:T(8,128)(2,1)S(1)}, bf16[4,64,768]{2,1,0:T(8,128)(2,1)S(1)}, u32[]{:S(2)}, u32[]{:S(2)}) collective-permute-start(bf16[4,64,768]{2,1,0:T(8,128)(2,1)S(1)} %bitcast.8), channel_id=1, source_target_pairs={{0,32},{32,64},{64,96},{96,128},{128,160},{160,192},{192,224},{224... | collective-permute-start | bytes 1179656 | tf_op jit(solution)/shard_map/ppermute | solution.py:37
  40.5 5.0 %collective-permute-done.5 = bf16[4,64,768]{2,1,0:T(8,128)(2,1)S(1)} collective-permute-done((bf16[4,64,768]{2,1,0:T(8,128)(2,1)S(1)}, bf16[4,64,768]{2,1,0:T(8,128)(2,1)S(1)}, u32[]{:S(2)}, u32[]{:S(2)}) %collective-permute-start.5) | collective-permute-done | bytes 393248 | tf_op jit(solution)/shard_map/ppermute | solution.py:238
  45.5 4.0 %collective-permute-done.4 = bf16[4,64,768]{2,1,0:T(8,128)(2,1)S(1)} collective-permute-done((bf16[4,64,768]{2,1,0:T(8,128)(2,1)S(1)}, bf16[4,64,768]{2,1,0:T(8,128)(2,1)S(1)}, u32[]{:S(2)}, u32[]{:S(2)}) %collective-permute-start.4) | collective-permute-done | bytes 393248 | tf_op jit(solution)/shard_map/ppermute | solution.py:37
  49.6 0.9 collective-permute-done.6
  50.5 0.0 copy-start.1
  50.5 0.2 pad_maximum_fusion.own_hbm
  50.7 0.0 copy-start
  50.7 1.9 %collective-permute-start.7 = (bf16[4,4,64,768]{3,2,1,0:T(8,128)(2,1)S(1)}, bf16[4,4,64,768]{3,2,1,0:T(8,128)(2,1)S(1)}, u32[]{:S(2)}, u32[]{:S(2)}) collective-permute-start(bf16[4,4,64,768]{3,2,1,0:T(8,128)(2,1)S(1)} %pad_maximum_fusion.own_hbm), channel_id=1, source_target_pairs={{0,8},{8,0},{1,9},{9,1},{2,10},{10,2},{3,11},{11,3},{4,12},{12,4},... | collective-permute-start | bytes 4718600 | tf_op jit(solution)/shard_map/ppermute | solution.py:37
  52.6 0.0 copy-done.1
  52.6 4.9 %collective-permute-start.1 = (bf16[256,256]{1,0:T(8,128)(2,1)S(1)}, bf16[256,256]{1,0:T(8,128)(2,1)S(1)}, u32[]{:S(2)}, u32[]{:S(2)}) collective-permute-start(bf16[256,256]{1,0:T(8,128)(2,1)S(1)} %copy-done.1), channel_id=1, source_target_pairs={{0,16},{8,24},{16,32},{24,40},{32,48},{40,56},{48,64},{56,72},{64,... | collective-permute-start | bytes 393224 | tf_op jit(solution)/shard_map/ppermute | solution.py:32
  57.6 2.1 %collective-permute-start = (bf16[256,256]{1,0:T(8,128)(2,1)S(1)}, bf16[256,256]{1,0:T(8,128)(2,1)S(1)}, u32[]{:S(2)}, u32[]{:S(2)}) collective-permute-start(bf16[256,256]{1,0:T(8,128)(2,1)S(1)} %copy-done.1), channel_id=1, source_target_pairs={{0,8},{8,16},{16,24},{24,32},{32,40},{40,48},{48,56},{56,64},{64,7... | collective-permute-start | bytes 393224 | tf_op jit(solution)/shard_map/ppermute | solution.py:32
  59.7 3.1 %collective-permute-done.1.kv2_ref = bf16[256,256]{1,0:T(8,128)(2,1)S(1)} collective-permute-done((bf16[256,256]{1,0:T(8,128)(2,1)S(1)}, bf16[256,256]{1,0:T(8,128)(2,1)S(1)}, u32[]{:S(2)}, u32[]{:S(2)}) %collective-permute-start.1) | collective-permute-done | bytes 131104 | tf_op jit(solution)/shard_map/ppermute | solution.py:32
  62.8 3.4 %collective-permute-done.kv1_ref = bf16[256,256]{1,0:T(8,128)(2,1)S(1)} collective-permute-done((bf16[256,256]{1,0:T(8,128)(2,1)S(1)}, bf16[256,256]{1,0:T(8,128)(2,1)S(1)}, u32[]{:S(2)}, u32[]{:S(2)}) %collective-permute-start) | collective-permute-done | bytes 131104 | tf_op jit(solution)/shard_map/ppermute | solution.py:32
  66.3 5.2 %attention.1 = (bf16[256,512]{1,0:T(8,128)(2,1)}, f32[256,256]{1,0:T(8,128)}, bf16[256,256]{1,0:T(8,128)(2,1)}, bf16[256,256]{1,0:T(8,128)(2,1)}) custom-call(s32[3,2,4]{2,1,0:T(2,128)} %bitcast.13, bf16[256,512]{1,0:T(8,128)(2,1)} %q_ref.1, bf16[256,512]{1,0:T(8,128)(2,1)} %do_ref.1, bf16[256,512]{1,0:T(8,128)(2,1)} %o_ref.1, f32[4,256]{1,0:T(4,128)} %lse_ref.1, ...), custom_call_target="tpu_custom_call" | custom-call | tf_op jit(solution)/shard_map/attention/pallas_call | solution.py:108
  71.4 1.9 %collective-permute-start.2 = (bf16[256,256]{1,0:T(8,128)(2,1)}, bf16[256,256]{1,0:T(8,128)(2,1)S(1)}, u32[]{:S(2)}, u32[]{:S(2)}) collective-permute-start(bf16[256,256]{1,0:T(8,128)(2,1)} %get-tuple-element.14), channel_id=1, source_target_pairs={{8,0},{16,8},{24,16},{32,24},{40,32},{48,40},{56,48},{64,56},{72,6... | collective-permute-start | bytes 393224 | tf_op jit(solution)/shard_map/ppermute | solution.py:32
  73.3 2.8 %collective-permute-start.3 = (bf16[256,256]{1,0:T(8,128)(2,1)}, bf16[256,256]{1,0:T(8,128)(2,1)S(1)}, u32[]{:S(2)}, u32[]{:S(2)}) collective-permute-start(bf16[256,256]{1,0:T(8,128)(2,1)} %get-tuple-element.15), channel_id=1, source_target_pairs={{16,0},{24,8},{32,16},{40,24},{48,32},{56,40},{64,48},{72,56},{80,... | collective-permute-start | bytes 393224 | tf_op jit(solution)/shard_map/ppermute | solution.py:32
  76.1 0.0 collective-permute-done.2
  76.2 6.7 %collective-permute-done.3 = bf16[256,256]{1,0:T(8,128)(2,1)S(1)} collective-permute-done((bf16[256,256]{1,0:T(8,128)(2,1)}, bf16[256,256]{1,0:T(8,128)(2,1)S(1)}, u32[]{:S(2)}, u32[]{:S(2)}) %collective-permute-start.3) | collective-permute-done | bytes 131104 | tf_op jit(solution)/shard_map/ppermute | solution.py:32
  82.8 1.0 add_convert_fusion
  83.9 1.0 pad_maximum_fusion.1
  84.8 12.9 %all-gather.a_hbm = bf16[512,768]{1,0:T(8,128)(2,1)} all-gather(bf16[256,768]{1,0:T(8,128)(2,1)S(1)} %pad_maximum_fusion.1), channel_id=2, replica_groups=mesh['zh'=4,'zl'=4,'xh'=2,'core'=2,'xl'=2,'y'=4] {'xh'}, dimensions={0}, use_global_device_ids=true | all-gather | bytes 1179648 | tf_op jit(solution)/shard_map/all_gather | solution.py:247
  97.8 0.0 copy-done
  97.8 0.0 collective-permute-done.7.other_ref
  97.8 7.4 %project.1 = bf16[16,256,256]{2,1,0:T(8,128)(2,1)} custom-call(bf16[512,768]{1,0:T(8,128)(2,1)} %all-gather.a_hbm, bf16[4,4,64,768]{3,2,1,0:T(8,128)(2,1)} %copy-done, bf16[4,4,64,768]{3,2,1,0:T(8,128)(2,1)S(1)} %collective-permute-done.7.other_ref), custom_call_target="tpu_custom_call" | custom-call | tf_op jit(solution)/shard_map/project/pallas_call | solution.py:165
  105.2 33.0 %all_to_all.5.in_ref = bf16[16,256,256]{2,1,0:T(8,128)(2,1)S(1)} all-to-all(bf16[16,256,256]{2,1,0:T(8,128)(2,1)} %project.1), channel_id=1, replica_groups=mesh['zh'=4,'zl'=4,'xh'=2,'core'=2,'xl'=2,'y'=4] {'xh','xl','y'}, dimensions={0} | all-to-all | bytes 4194304 | tf_op jit(solution)/shard_map/all_to_all | solution.py:249
  138.2 1.0 total.1
Async XLA Ops:
  31.1 14.5 %collective-permute-start.5 = (bf16[4,64,768]{2,1,0:T(8,128)(2,1)S(1)}, bf16[4,64,768]{2,1,0:T(8,128)(2,1)S(1)}, u32[]{:S(2)}, u32[]{:S(2)}) collective-permute-start(bf16[4,64,768]{2,1,0:T(8,128)(2,1)S(1)} %bitcast.6), channel_id=1, source_target_pairs={{64,0},{480,32},{128,64},{32,96},{192,128},{96,160},{256,192},{160... | collective-permute-start | bytes 1179656 | tf_op jit(solution)/shard_map/ppermute | solution.py:238
  34.6 14.9 %collective-permute-start.4 = (bf16[4,64,768]{2,1,0:T(8,128)(2,1)S(1)}, bf16[4,64,768]{2,1,0:T(8,128)(2,1)S(1)}, u32[]{:S(2)}, u32[]{:S(2)}) collective-permute-start(bf16[4,64,768]{2,1,0:T(8,128)(2,1)S(1)} %bitcast.7), channel_id=1, source_target_pairs={{0,480},{32,0},{64,32},{96,64},{128,96},{160,128},{192,160},{224,1... | collective-permute-start | bytes 1179656 | tf_op jit(solution)/shard_map/ppermute | solution.py:37
  37.7 12.8 %collective-permute-start.6 = (bf16[4,64,768]{2,1,0:T(8,128)(2,1)S(1)}, bf16[4,64,768]{2,1,0:T(8,128)(2,1)S(1)}, u32[]{:S(2)}, u32[]{:S(2)}) collective-permute-start(bf16[4,64,768]{2,1,0:T(8,128)(2,1)S(1)} %bitcast.8), channel_id=1, source_target_pairs={{0,32},{32,64},{64,96},{96,128},{128,160},{160,192},{192,224},{224... | collective-permute-start | bytes 1179656 | tf_op jit(solution)/shard_map/ppermute | solution.py:37
  50.5 2.1 %copy-start.1 = (bf16[256,256]{1,0:T(8,128)(2,1)S(1)}, bf16[256,256]{1,0:T(8,128)(2,1)}, u32[]{:S(2)}) copy-start(bf16[256,256]{1,0:T(8,128)(2,1)} %get-tuple-element.11.kv0_ref) | copy-start | bytes 393220
  50.7 47.1 %copy-start = (bf16[4,4,64,768]{3,2,1,0:T(8,128)(2,1)}, bf16[4,4,64,768]{3,2,1,0:T(8,128)(2,1)S(1)}, u32[]{:S(2)}) copy-start(bf16[4,4,64,768]{3,2,1,0:T(8,128)(2,1)S(1)} %pad_maximum_fusion.own_hbm) | copy-start | bytes 4718596
  50.7 47.1 %collective-permute-start.7 = (bf16[4,4,64,768]{3,2,1,0:T(8,128)(2,1)S(1)}, bf16[4,4,64,768]{3,2,1,0:T(8,128)(2,1)S(1)}, u32[]{:S(2)}, u32[]{:S(2)}) collective-permute-start(bf16[4,4,64,768]{3,2,1,0:T(8,128)(2,1)S(1)} %pad_maximum_fusion.own_hbm), channel_id=1, source_target_pairs={{0,8},{8,0},{1,9},{9,1},{2,10},{10,2},{3,11},{11,3},{4,12},{12,4},... | collective-permute-start | bytes 4718600 | tf_op jit(solution)/shard_map/ppermute | solution.py:37
  52.6 10.2 %collective-permute-start.1 = (bf16[256,256]{1,0:T(8,128)(2,1)S(1)}, bf16[256,256]{1,0:T(8,128)(2,1)S(1)}, u32[]{:S(2)}, u32[]{:S(2)}) collective-permute-start(bf16[256,256]{1,0:T(8,128)(2,1)S(1)} %copy-done.1), channel_id=1, source_target_pairs={{0,16},{8,24},{16,32},{24,40},{32,48},{40,56},{48,64},{56,72},{64,... | collective-permute-start | bytes 393224 | tf_op jit(solution)/shard_map/ppermute | solution.py:32
  57.6 8.7 %collective-permute-start = (bf16[256,256]{1,0:T(8,128)(2,1)S(1)}, bf16[256,256]{1,0:T(8,128)(2,1)S(1)}, u32[]{:S(2)}, u32[]{:S(2)}) collective-permute-start(bf16[256,256]{1,0:T(8,128)(2,1)S(1)} %copy-done.1), channel_id=1, source_target_pairs={{0,8},{8,16},{16,24},{24,32},{32,40},{40,48},{48,56},{56,64},{64,7... | collective-permute-start | bytes 393224 | tf_op jit(solution)/shard_map/ppermute | solution.py:32
  71.4 4.7 %collective-permute-start.2 = (bf16[256,256]{1,0:T(8,128)(2,1)}, bf16[256,256]{1,0:T(8,128)(2,1)S(1)}, u32[]{:S(2)}, u32[]{:S(2)}) collective-permute-start(bf16[256,256]{1,0:T(8,128)(2,1)} %get-tuple-element.14), channel_id=1, source_target_pairs={{8,0},{16,8},{24,16},{32,24},{40,32},{48,40},{56,48},{64,56},{72,6... | collective-permute-start | bytes 393224 | tf_op jit(solution)/shard_map/ppermute | solution.py:32
  73.3 9.5 %collective-permute-start.3 = (bf16[256,256]{1,0:T(8,128)(2,1)}, bf16[256,256]{1,0:T(8,128)(2,1)S(1)}, u32[]{:S(2)}, u32[]{:S(2)}) collective-permute-start(bf16[256,256]{1,0:T(8,128)(2,1)} %get-tuple-element.15), channel_id=1, source_target_pairs={{16,0},{24,8},{32,16},{40,24},{48,32},{56,40},{64,48},{72,56},{80,... | collective-permute-start | bytes 393224 | tf_op jit(solution)/shard_map/ppermute | solution.py:32
